TPU v7x, 32 devices: a whole 2x2x4 slice. The times are simulated.
32 devices in a mesh: box: 16 (over z, y, x), dir: 2 (over core).
Axes of the slice: x: 2, y: 2, z: 4, core: 2. Of those that a mesh axis runs over, the one named last changes fastest.
Arguments:
- sources: bfloat16 [64, 2, 32, 256], P('box'), may hold values from -6 to 6
- encode: bfloat16 [2, 1024, 256], P(None, 'dir'), may hold values from -0.375 to 0.375
- kernel: float32 [1024, 2, 4, 128], P(('dir', 'box')), may hold values from -0.5 to 0.5
- decode: bfloat16 [2, 1024, 256], P(None, 'dir'), may hold values from -0.1875 to 0.1875
- near_blocks: bfloat16 [64, 28, 2, 256, 256], P('box', 'dir'), may hold values from -0.078125 to 0.078125
- near_list: int32 [64, 28], P('box', 'dir'), may hold values from 0 to 63, as said below
- near_mask: int32 [64, 28], P('box', 'dir'), may hold values from 0 to 1, as said below
- box_cell: int32 [64], replicated, may hold values from 0 to 63, as said below
Outputs:
- product: float32 [64, 2, 32, 256], P('box', None, None, 'dir')
Inputs may be any that keep to these rules, and one draw needn't show every extreme that they name: A permutation of the cells: box b lies in cell box_cell[b] = (ix * 8 + iy) * 4 + iz of the 2 x 8 x 4 grid. Where near_mask[b, s] is 1, near_list[b, s] is the box whose cell differs from box b's cell by -1, 0 or 1 along each dimension, each such box named in one slot of b (b itself included); elsewhere any box. `near_mask`: 1 exactly where the slot names a cell inside the grid; at least one slot of every box is 0.
All inputs are finite; a program needn't handle non-finite values.
Results may differ from a plain program's by a relative error of at most 0.0027.
Values may be sent and summed in bfloat16 or wider, within the bound.
No kernel may reach another device: no remote copies, remote signals or barrier semaphores. Data moves between devices by JAX's collectives and lax.ppermute only.
A program may use at most 128 MiB of HBM per device.

v0:
```python
import functools
import math

import jax
import jax.numpy as jnp
import numpy as np
from jax import lax
from jax.experimental import pallas as pl
from jax.experimental.pallas import tpu as pltpu
from jax.sharding import PartitionSpec as P


GY = 8
GZ = 4
LANES = 128

F32 = jnp.float32
BF16 = jnp.bfloat16


def dot_nt(left, right):
    return lax.dot_general(left, right, (((1,), (1,)), ((), ())), preferred_element_type=F32)


def dot_nn(left, right):
    return lax.dot_general(left, right, (((1,), (0,)), ((), ())), preferred_element_type=F32)


def split(value):
    high = value.astype(BF16)
    return high, (value - high.astype(F32)).astype(BF16)


def plane_table(points_y, points_z):
    freq = np.arange(4 * GY * GZ)
    turns = np.outer(freq // (2 * GZ), points_y) % (2 * GY) / (2 * GY)
    turns = turns + np.outer(freq % (2 * GZ), points_z) % (2 * GZ) / (2 * GZ)
    cosine, sine = np.cos(2.0 * math.pi * turns), np.sin(2.0 * math.pi * turns)
    table = np.block([[cosine, sine], [-sine, cosine]]).astype(np.float32)
    high = table.astype(BF16)
    return high, (table - high.astype(np.float32)).astype(BF16)


def part_rows(box, rhs):
    start = 2 * box * rhs
    return slice(start, start + rhs), slice(start + rhs, start + 2 * rhs)


def encode_kernel(rhs, group, src_hbm, enc_hbm, out_ref, share_ref, src_ref, enc_ref, coded_ref, sem):
    copies = [
        pltpu.make_async_copy(src_hbm, src_ref, sem.at[0]),
        pltpu.make_async_copy(enc_hbm.at[0], enc_ref.at[0], sem.at[1]),
        pltpu.make_async_copy(enc_hbm.at[1], enc_ref.at[1], sem.at[2]),
    ]
    for copy in copies:
        copy.start()
    copies[0].wait()
    src = src_ref[...]
    part = src.shape[0] // lax.axis_size("dir")
    share_ref[...] = src_ref[pl.ds(pl.multiple_of(lax.axis_index("dir") * part, part), part), :]
    copies[1].wait()
    with_re = dot_nt(src, enc_ref[0])
    copies[2].wait()
    with_im = dot_nt(src, enc_ref[1])
    rows = src.shape[0] // rhs
    pieces = LANES // group
    for block in range(coded_ref.shape[0]):
        cols = slice(block * LANES, (block + 1) * LANES)
        for box in range(rows // 2):
            re, im = part_rows(box, rhs)
            coded_ref[block, re, :] = with_re[re, cols] - with_im[im, cols]
            coded_ref[block, im, :] = with_re[im, cols] + with_im[re, cols]
    for block in range(coded_ref.shape[0]):
        flat = coded_ref.at[block]
        for tile in range(rhs // pieces):
            parts = [flat[pl.ds(tile * pieces + n, rows, stride=rhs), :] for n in range(pieces)]
            for slot in range(pieces):
                lanes = slice(slot * group, (slot + 1) * group)
                out_ref[block * pieces + slot, :, tile * LANES : (tile + 1) * LANES] = jnp.concatenate(
                    [part[:, lanes] for part in parts], axis=1
                ).astype(BF16)


def table_kernel(grid_x, parts, box_hbm, kern_hbm, cell_hbm, full_hbm, fwd_ref, inv_ref, spec_ref, box_ref, kern_ref, cell_ref, full_ref, sem):
    copies = [
        pltpu.make_async_copy(box_hbm, box_ref, sem.at[0]),
        pltpu.make_async_copy(cell_hbm, cell_ref, sem.at[1]),
        pltpu.make_async_copy(kern_hbm, kern_ref, sem.at[2]),
        pltpu.make_async_copy(full_hbm, full_ref, sem.at[3]),
    ]
    for copy in copies:
        copy.start()
    full_hi, full_lo = full_ref.at[0], full_ref.at[1]
    cell_hi, cell_lo = cell_ref.at[0], cell_ref.at[1]
    plane = full_hi.shape[0] // 2
    cells = GY * GZ
    count = box_ref.shape[1]
    boxes = count * parts
    copies[0].wait()
    copies[1].wait()
    same = lax.broadcasted_iota(jnp.int32, (boxes, count), 0) // parts == lax.broadcasted_iota(jnp.int32, (boxes, count), 1)
    cell_col = jnp.sum(jnp.where(same, box_ref[...], 0), axis=1, keepdims=True)
    spread = jnp.where(same, 1.0, 0.0).astype(BF16)
    cell_row = dot_nt(jnp.broadcast_to(box_ref[...], (8, count)).astype(BF16), spread)[:1].astype(jnp.int32)
    down = lax.broadcasted_iota(jnp.int32, (2 * cells, boxes), 0)
    part_row = lax.broadcasted_iota(jnp.int32, (2 * cells, boxes), 1) % 2
    across = lax.broadcasted_iota(jnp.int32, (boxes, 2 * cells), 1)
    part_col = lax.broadcasted_iota(jnp.int32, (boxes, 2 * cells), 0) % 2
    for x in range(grid_x):
        hit = (cell_row - x * cells + part_row * cells == down) & (cell_row // cells == x)
        place = jnp.where(hit, 1.0, 0.0).astype(BF16)
        fwd_ref[x, :, :boxes] = dot_nn(cell_hi[...], place).astype(BF16)
        fwd_ref[x, :, boxes:] = dot_nn(cell_lo[...], place).astype(BF16)
        hit = (cell_col - x * cells + part_col * cells == across) & (cell_col // cells == x)
        place = jnp.where(hit, 1.0 / plane, 0.0).astype(BF16)
        inv_ref[x, 0] = dot_nt(place, cell_hi[...]).astype(BF16)
        inv_ref[x, 1] = dot_nt(place, cell_lo[...]).astype(BF16)
    point = lax.broadcasted_iota(jnp.int32, (1, 2 * plane), 1) % plane
    off_y, off_z = point // (2 * GZ), point % (2 * GZ)
    close = ((off_y <= 1) | (off_y == 2 * GY - 1)) & ((off_z <= 1) | (off_z == 2 * GZ - 1))
    keep = jnp.where(close, 0.0, 1.0)
    copies[2].wait()
    copies[3].wait()
    repeat = LANES // kern_ref.shape[0]
    double_x = kern_ref.shape[2]
    for off in range(double_x):
        if off == grid_x:
            continue
        kept = jnp.concatenate([kern_ref[:, 0, off, :], kern_ref[:, 1, off, :]], axis=1)
        if off <= 1 or off == double_x - 1:
            kept = kept * keep
        high, low = split(kept)
        high = jnp.concatenate([high] * repeat, axis=0)
        low = jnp.concatenate([low] * repeat, axis=0)
        spec_ref[off] = dot_nt(full_hi[...], high) + dot_nt(full_hi[...], low) + dot_nt(full_lo[...], high)


def far_kernel(grid_x, coded_ref, fwd_ref, inv_ref, spec_ref, out_ref):
    owners, rows, width = coded_ref.shape
    plane = spec_ref.shape[1] // 2
    double_x = spec_ref.shape[0]
    step = min(2 * LANES, width)
    for start in range(0, width, step):
        cols = slice(start, start + step)
        coded = coded_ref[:, :, cols].reshape(owners * rows, step)
        coded = jnp.concatenate([coded, coded], axis=0)
        data = [dot_nn(fwd_ref[x], coded) for x in range(grid_x)]
        total = None
        for x in range(grid_x):
            tiles = []
            for tile in range(step // LANES):
                lanes = slice(tile * LANES, (tile + 1) * LANES)
                re = im = None
                for s in range(grid_x):
                    off = (x - s) % double_x
                    s_re, s_im = spec_ref[off, :plane], spec_ref[off, plane:]
                    d_re, d_im = data[s][:plane, lanes], data[s][plane:, lanes]
                    p_re = d_re * s_re - d_im * s_im
                    p_im = d_re * s_im + d_im * s_re
                    re = p_re if re is None else re + p_re
                    im = p_im if im is None else im + p_im
                tiles.append(jnp.concatenate([re, im], axis=0))
            high, low = split(jnp.concatenate(tiles, axis=1))
            term = dot_nn(inv_ref[x, 0], high) + dot_nn(inv_ref[x, 0], low) + dot_nn(inv_ref[x, 1], high)
            total = term if total is None else total + term
        out_ref[:, :, cols] = total.astype(BF16).reshape(owners, rows, step)


def near_kernel(share, mine, list_ref, mask_ref, src_ref, blocks_ref, base_ref, out_ref, blk, acc, sem):
    boxes, slots = blocks_ref.shape[0], blocks_ref.shape[1]
    unknowns = blocks_ref.shape[4]
    me, side = lax.axis_index("box"), lax.axis_index("dir")
    wanted = side if mine else 1 - side

    def used(box, slot):
        return (mask_ref[box, slot] != 0) & (list_ref[box, slot] % boxes // share == wanted)

    def block_copy(box, slot):
        n = box * slots + slot
        return pltpu.make_async_copy(blocks_ref.at[box, slot], blk.at[n], sem.at[n])

    for box in range(boxes):

        @pl.loop(0, slots)
        def _(slot):
            @pl.when(used(box, slot))
            def _():
                block_copy(box, slot).start()

    half = src_ref.shape[2] // 2
    for box in range(boxes):
        acc[...] = jnp.zeros_like(acc)

        @pl.loop(0, slots)
        def _(slot):
            @pl.when(used(box, slot))
            def _():
                block_copy(box, slot).wait()
                n = box * slots + slot
                source = list_ref[box, slot]
                vector = src_ref[(source // boxes) ^ me, source % share]
                acc[...] += jnp.concatenate([dot_nt(vector, blk[n, 0]), dot_nt(vector, blk[n, 1])], axis=1)

        re, im = slice(0, half), slice(half, 2 * half)
        with_re, with_im = acc[:, :unknowns], acc[:, unknowns:]
        near_re = with_re[re] - with_im[im]
        near_im = with_re[im] + with_im[re]
        rows_re, rows_im = part_rows(box, half)
        if not mine:
            near_re = near_re + base_ref[rows_re, :]
            near_im = near_im + base_ref[rows_im, :]
        out_ref[rows_re, :] = near_re
        out_ref[rows_im, :] = near_im


def decode_kernel(rhs, group, far_ref, dec_ref, near_ref, own_ref, other_ref, wide, total):
    _, rows, width = far_ref.shape
    pieces = LANES // group
    for block in range(wide.shape[0]):
        flat = wide.at[block]
        for tile in range(width // LANES):
            cols = slice(tile * LANES, (tile + 1) * LANES)
            parts = [far_ref[block * pieces + slot, :, cols].astype(F32) for slot in range(pieces)]
            for n in range(pieces):
                lanes = slice(n * group, (n + 1) * group)
                flat[pl.ds(tile * pieces + n, rows, stride=rhs), :] = jnp.concatenate(
                    [part[:, lanes] for part in parts], axis=1
                )
    fields = jnp.concatenate([wide[block].astype(BF16) for block in range(wide.shape[0])], axis=1)
    with_re = dot_nn(fields, dec_ref[0])
    with_im = dot_nn(fields, dec_ref[1])
    for box in range(rows // 2):
        re, im = part_rows(box, rhs)
        total[re, :] = near_ref[re, :] + (with_re[re] - with_im[im])
        total[im, :] = near_ref[im, :] + (with_re[im] + with_im[re])
    half = total.shape[1] // 2
    first = lax.axis_index("dir") == 0
    left, right = total[:, :half], total[:, half:]
    own_ref[...] = jnp.where(first, left, right)
    other_ref[...] = jnp.where(first, right, left)


def join_kernel(*refs):
    for n, ref in enumerate(refs[:-1]):
        refs[-1][:, n] = ref[...]


def join(pieces):
    shape = pieces[0].shape
    joined = pl.pallas_call(
        join_kernel,
        out_shape=pltpu.VMEM((shape[0], len(pieces)) + shape[1:], pieces[0].dtype),
        in_specs=[vmem()] * len(pieces),
        out_specs=vmem(),
        compiler_params=budget(4),
        name="join",
    )(*pieces)
    return joined.reshape((-1,) + shape[1:])


def gather_shares(share):
    size = lax.axis_size("box")
    held = share[None]
    low = size
    while low > 1:
        fan = 4 if low % 4 == 0 else 2
        low //= fan
        moved = [held]
        for delta in range(1, fan):
            moved.append(lax.ppermute(held, "box", [(i, i ^ (delta * low)) for i in range(size)]))
        held = join(moved)
    return held


def budget(mebibytes):
    return pltpu.CompilerParams(vmem_limit_bytes=mebibytes << 20)


def stay(array):
    return pltpu.with_memory_space_constraint(array, pltpu.HBM)


def vmem():
    return pl.BlockSpec(memory_space=pltpu.VMEM)


def smem():
    return pl.BlockSpec(memory_space=pltpu.SMEM)


def hbm():
    return pl.BlockSpec(memory_space=pltpu.HBM)


def whole_product(sources, encode, kernel, decode, near_blocks, near_list, near_mask, box_cell):
    owners, sides = lax.axis_size("box"), lax.axis_size("dir")
    per_box, parts, rhs, unknowns = sources.shape
    group_dirs, _, double_x, plane = kernel.shape
    side_dirs = encode.shape[1]
    grid_x = double_x // 2
    rows = per_box * parts
    width = rhs * group_dirs
    boxes = box_cell.shape[0]

    share = per_box // sides
    coded, own_share = pl.pallas_call(
        functools.partial(encode_kernel, rhs, group_dirs),
        out_shape=(
            pltpu.VMEM((owners, rows, width), BF16),
            pltpu.VMEM((share * parts * rhs, unknowns), BF16),
        ),
        in_specs=[hbm(), hbm()],
        out_specs=(vmem(),) * 2,
        scratch_shapes=[
            pltpu.VMEM((rows * rhs, unknowns), BF16),
            pltpu.VMEM(encode.shape, BF16),
            pltpu.VMEM((side_dirs // LANES, rows * rhs, LANES), F32),
            pltpu.SemaphoreType.DMA((3,)),
        ],
        compiler_params=budget(8),
        name="encode",
    )(stay(sources.reshape(rows * rhs, unknowns)), stay(encode))
    arrived = lax.all_to_all(coded, "box", split_axis=0, concat_axis=0, tiled=True)
    mine = gather_shares(own_share.reshape(share, parts * rhs, unknowns))
    theirs = lax.ppermute(mine, "dir", [(i, 1 - i) for i in range(sides)])

    cell = np.arange(GY * GZ)
    cell_hi, cell_lo = plane_table(cell // GZ, cell % GZ)
    point = np.arange(plane)
    full_hi, full_lo = plane_table(point // (2 * GZ), point % (2 * GZ))
    constants = (np.stack([cell_hi, cell_lo]), np.stack([full_hi, full_lo]))
    forward, inverse, spectrum = pl.pallas_call(
        functools.partial(table_kernel, grid_x, parts),
        out_shape=(
            pltpu.VMEM((grid_x, 2 * plane, 2 * parts * boxes), BF16),
            pltpu.VMEM((grid_x, 2, parts * boxes, 2 * plane), BF16),
            pltpu.VMEM((double_x, 2 * plane, LANES), F32),
        ),
        in_specs=[hbm()] * 4,
        out_specs=(vmem(),) * 3,
        scratch_shapes=[
            pltpu.VMEM((1, boxes), jnp.int32),
            pltpu.VMEM(kernel.shape, F32),
            pltpu.VMEM(constants[0].shape, BF16),
            pltpu.VMEM(constants[1].shape, BF16),
            pltpu.SemaphoreType.DMA((4,)),
        ],
        compiler_params=budget(24),
        name="tables",
    )(stay(box_cell[None, :]), stay(kernel), *[stay(jnp.asarray(table)) for table in constants])

    far = pl.pallas_call(
        functools.partial(far_kernel, grid_x),
        out_shape=pltpu.VMEM((owners, rows, width), BF16),
        in_specs=[vmem()] * 4,
        out_specs=vmem(),
        compiler_params=budget(8),
        name="far",
    )(arrived, forward, inverse, spectrum)
    returned = lax.all_to_all(far, "box", split_axis=0, concat_axis=0, tiled=True)


    slots = near_list.shape[1]

    def near(is_mine, vectors, base):
        return pl.pallas_call(
            functools.partial(near_kernel, share, is_mine),
            out_shape=pltpu.VMEM((rows * rhs, unknowns), F32),
            in_specs=[smem(), smem(), vmem(), hbm(), vmem()],
            out_specs=vmem(),
            scratch_shapes=[
                pltpu.VMEM((per_box * slots, parts, unknowns, unknowns), BF16),
                pltpu.VMEM((parts * rhs, parts * unknowns), F32),
                pltpu.SemaphoreType.DMA((per_box * slots,)),
            ],
            compiler_params=budget(20),
            name="near_mine" if is_mine else "near_theirs",
        )(stay(near_list), stay(near_mask), vectors, stay(near_blocks), base)

    near_part = near(True, mine, own_share)
    near_part = near(False, theirs, near_part)

    half = unknowns // sides
    own, other = pl.pallas_call(
        functools.partial(decode_kernel, rhs, group_dirs),
        out_shape=(pltpu.VMEM((rows * rhs, half), F32),) * 2,
        in_specs=[vmem(), vmem(), vmem()],
        out_specs=(vmem(),) * 2,
        scratch_shapes=[
            pltpu.VMEM((side_dirs // LANES, rows * rhs, LANES), F32),
            pltpu.VMEM((rows * rhs, unknowns), F32),
        ],
        compiler_params=budget(8),
        name="decode",
    )(returned, decode, near_part)
    swapped = lax.ppermute(other, "dir", [(i, 1 - i) for i in range(sides)])
    return (own + swapped).reshape(per_box, parts, rhs, half)


def solution(mesh):
    in_specs = (
        P("box", None, None, None),
        P(None, "dir", None),
        P(("dir", "box"), None, None, None),
        P(None, "dir", None),
        P("box", "dir", None, None, None),
        P("box", "dir"),
        P("box", "dir"),
        P(),
    )
    out_specs = P("box", None, None, "dir")
    return jax.shard_map(whole_product, mesh=mesh, in_specs=in_specs, out_specs=out_specs, check_vma=False)
```

profile of v0, /device:TPU:27, one launch (start us, length us, event | category | flops | bytes accessed | tf_op | source)
XLA Modules:
  0.0 65.9 jit_solution(14502091024435054099)
XLA Ops:
  0.0 2.6 %encode.1 = (bf16[16,8,1024]{2,1,0:T(8,128)(2,1)}, bf16[128,256]{1,0:T(8,128)(2,1)S(1)}) custom-call(bf16[256,256]{1,0:T(8,128)(2,1)} %bitcast.16, bf16[2,512,256]{2,1,0:T(8,128)(2,1)} %enc_hbm.1), custom_call_target="tpu_custom_call" | custom-call | tf_op jit(solution)/shard_map/encode/pallas_call | solution.py:306
  2.6 0.2 collective-permute-start
  2.9 3.3 %collective-permute-start.2 = (bf16[1,2,64,256]{3,2,1,0:T(8,128)(2,1)S(1)}, bf16[1,2,64,256]{3,2,1,0:T(8,128)(2,1)S(1)}, u32[]{:S(2)}, u32[]{:S(2)}) collective-permute-start(bf16[1,2,64,256]{3,2,1,0:T(8,128)(2,1)S(1)} %bitcast.14), channel_id=1, source_target_pairs={{0,24},{2,26},{4,28},{6,30},{8,16},{10,18},{12,20},{14,22},{16,8},... | collective-permute-start | bytes 196616 | tf_op jit(solution)/shard_map/ppermute | solution.py:270
  6.3 0.7 %collective-permute-done.1.refs_2_ = bf16[1,2,64,256]{3,2,1,0:T(8,128)(2,1)S(1)} collective-permute-done((bf16[1,2,64,256]{3,2,1,0:T(8,128)(2,1)S(1)}, bf16[1,2,64,256]{3,2,1,0:T(8,128)(2,1)S(1)}, u32[]{:S(2)}, u32[]{:S(2)}) %collective-permute-start.1) | collective-permute-done | bytes 65568 | tf_op jit(solution)/shard_map/ppermute | solution.py:270
  7.0 1.8 %collective-permute-done.2.refs_3_ = bf16[1,2,64,256]{3,2,1,0:T(8,128)(2,1)S(1)} collective-permute-done((bf16[1,2,64,256]{3,2,1,0:T(8,128)(2,1)S(1)}, bf16[1,2,64,256]{3,2,1,0:T(8,128)(2,1)S(1)}, u32[]{:S(2)}, u32[]{:S(2)}) %collective-permute-start.2) | collective-permute-done | bytes 65568 | tf_op jit(solution)/shard_map/ppermute | solution.py:270
  8.8 0.3 collective-permute-start.3
  9.1 1.2 %collective-permute-start.4 = (bf16[4,2,64,256]{3,2,1,0:T(8,128)(2,1)S(1)}, bf16[4,2,64,256]{3,2,1,0:T(8,128)(2,1)S(1)}, u32[]{:S(2)}, u32[]{:S(2)}) collective-permute-start(bf16[4,2,64,256]{3,2,1,0:T(8,128)(2,1)S(1)} %bitcast.9), channel_id=1, source_target_pairs={{0,4},{2,6},{4,0},{6,2},{8,12},{10,14},{12,8},{14,10},{16,20},{18,... | collective-permute-start | bytes 786440 | tf_op jit(solution)/shard_map/ppermute | solution.py:270
  10.3 1.2 %collective-permute-start.5 = (bf16[4,2,64,256]{3,2,1,0:T(8,128)(2,1)S(1)}, bf16[4,2,64,256]{3,2,1,0:T(8,128)(2,1)S(1)}, u32[]{:S(2)}, u32[]{:S(2)}) collective-permute-start(bf16[4,2,64,256]{3,2,1,0:T(8,128)(2,1)S(1)} %bitcast.10), channel_id=1, source_target_pairs={{0,6},{2,4},{4,2},{6,0},{8,14},{10,12},{12,10},{14,8},{16,22},{18,... | collective-permute-start | bytes 786440 | tf_op jit(solution)/shard_map/ppermute | solution.py:270
  11.5 2.6 %collective-permute-done.3.refs_1_ = bf16[4,2,64,256]{3,2,1,0:T(8,128)(2,1)S(1)} collective-permute-done((bf16[4,2,64,256]{3,2,1,0:T(8,128)(2,1)S(1)}, bf16[4,2,64,256]{3,2,1,0:T(8,128)(2,1)S(1)}, u32[]{:S(2)}, u32[]{:S(2)}) %collective-permute-start.3) | collective-permute-done | bytes 262176 | tf_op jit(solution)/shard_map/ppermute | solution.py:270
  14.0 0.3 collective-permute-done.4.refs_2_
  14.3 5.6 %collective-permute-done.5.refs_3_ = bf16[4,2,64,256]{3,2,1,0:T(8,128)(2,1)S(1)} collective-permute-done((bf16[4,2,64,256]{3,2,1,0:T(8,128)(2,1)S(1)}, bf16[4,2,64,256]{3,2,1,0:T(8,128)(2,1)S(1)}, u32[]{:S(2)}, u32[]{:S(2)}) %collective-permute-start.5) | collective-permute-done | bytes 262176 | tf_op jit(solution)/shard_map/ppermute | solution.py:270
  19.9 0.1 join.3
  20.0 4.3 %collective-permute-start.6 = (bf16[16,2,64,256]{3,2,1,0:T(8,128)(2,1)S(1)}, bf16[16,2,64,256]{3,2,1,0:T(8,128)(2,1)S(1)}, u32[]{:S(2)}, u32[]{:S(2)}) collective-permute-start(bf16[16,2,64,256]{3,2,1,0:T(8,128)(2,1)S(1)} %bitcast.6), channel_id=1, source_target_pairs={{0,1},{1,0},{2,3},{3,2},{4,5},{5,4},{6,7},{7,6},{8,9},{9,8},{10,11... | collective-permute-start | bytes 3145736 | tf_op jit(solution)/shard_map/ppermute | solution.py:325
  24.3 6.8 %all-to-all-start = ((bf16[16,8,1024]{2,1,0:T(8,128)(2,1)}), bf16[16,8,1024]{2,1,0:T(8,128)(2,1)S(1)}, u32[]{:S(2)}, u32[]{:S(2)}) async-start(bf16[16,8,1024]{2,1,0:T(8,128)(2,1)} %get-tuple-element.12), calls=%async_computation | async-start | bytes 524288 | tf_op jit(solution)/shard_map/all_to_all | solution.py:323
  31.1 1.9 %tables.1 = (bf16[2,256,256]{2,1,0:T(8,128)(2,1)S(1)}, bf16[2,2,128,256]{3,2,1,0:T(8,128)(2,1)S(1)}, f32[4,256,128]{2,1,0:T(8,128)S(1)}) custom-call(s32[1,64]{1,0:T(1,128)} %bitcast.17, f32[32,2,4,128]{3,2,1,0:T(4,128)} %kern_hbm.1, bf16[2,256,64]{2,1,0:T(8,128)(2,1)} %constant.4.clone.cell_hbm, bf16[2,256,256]{2,1,0:T(8,128)(2,1)} %constant.5.clone.full_hbm), custom_call_target="tpu_custom_call" | custom-call | tf_op jit(solution)/shard_map/tables/pallas_call | solution.py:332
  33.0 5.0 %all-to-all-done.coded_ref = bf16[16,8,1024]{2,1,0:T(8,128)(2,1)S(1)} async-done(((bf16[16,8,1024]{2,1,0:T(8,128)(2,1)}), bf16[16,8,1024]{2,1,0:T(8,128)(2,1)S(1)}, u32[]{:S(2)}, u32[]{:S(2)}) %all-to-all-start) | async-done | bytes 262176 | tf_op jit(solution)/shard_map/all_to_all | solution.py:323
  38.0 2.4 %far.1 = bf16[16,8,1024]{2,1,0:T(8,128)(2,1)} custom-call(bf16[16,8,1024]{2,1,0:T(8,128)(2,1)S(1)} %all-to-all-done.coded_ref, bf16[2,256,256]{2,1,0:T(8,128)(2,1)S(1)} %get-tuple-element.13.fwd_ref, bf16[2,2,128,256]{3,2,1,0:T(8,128)(2,1)S(1)} %get-tuple-element.14.inv_ref, f32[4,256,128]{2,1,0:T(8,128)S(1)} %get-tuple-element.15.spec_ref), custom_call_target="tpu_custom_call" | custom-call | tf_op jit(solution)/shard_map/far/pallas_call | solution.py:352
  40.4 6.1 %all-to-all-start.1 = ((bf16[16,8,1024]{2,1,0:T(8,128)(2,1)}), bf16[16,8,1024]{2,1,0:T(8,128)(2,1)S(1)}, u32[]{:S(2)}, u32[]{:S(2)}) async-start(bf16[16,8,1024]{2,1,0:T(8,128)(2,1)} %far.1), calls=%async_computation.1 | async-start | bytes 524288 | tf_op jit(solution)/shard_map/all_to_all | solution.py:360
  46.5 6.2 %near_mine.1.base_ref = f32[256,256]{1,0:T(8,128)S(1)} custom-call(s32[4,14]{1,0:T(4,128)} %list_ref.3, s32[4,14]{1,0:T(4,128)} %mask_ref.3, bf16[16,2,64,256]{3,2,1,0:T(8,128)(2,1)S(1)} %bitcast.7, bf16[4,14,2,256,256]{4,3,2,1,0:T(8,128)(2,1)} %blocks_ref.3, bf16[128,256]{1,0:T(8,128)(2,1)S(1)} %get-tuple-element.16.base_ref), custom_call_target="tpu_custom_call" | custom-call | tf_op jit(solution)/shard_map/near_mine/pallas_call | solution.py:366
  52.7 5.3 %near_theirs.1.near_ref = f32[256,256]{1,0:T(8,128)S(1)} custom-call(s32[4,14]{1,0:T(4,128)} %list_ref.3, s32[4,14]{1,0:T(4,128)} %mask_ref.3, bf16[16,2,64,256]{3,2,1,0:T(8,128)(2,1)S(1)} %collective-permute-done.6.src_ref, bf16[4,14,2,256,256]{4,3,2,1,0:T(8,128)(2,1)} %blocks_ref.3, f32[256,256]{1,0:T(8,128)S(1)} %near_mine.1.base_ref), custom_call_target="tpu_custom_call" | custom-call | tf_op jit(solution)/shard_map/near_theirs/pallas_call | solution.py:366
  57.9 0.7 %decode.1 = (f32[256,128]{1,0:T(8,128)S(1)}, f32[256,128]{1,0:T(8,128)S(1)}) custom-call(bf16[16,8,1024]{2,1,0:T(8,128)(2,1)S(1)} %all-to-all-done.1.far_ref, bf16[2,512,256]{2,1,0:T(8,128)(2,1)S(1)} %copy-done, f32[256,256]{1,0:T(8,128)S(1)} %near_theirs.1.near_ref), custom_call_target="tpu_custom_call" | custom-call | tf_op jit(solution)/shard_map/decode/pallas_call | solution.py:384
  58.6 5.6 %collective-permute-start.7 = (f32[256,128]{1,0:T(8,128)S(1)}, f32[256,128]{1,0:T(8,128)S(1)}, u32[]{:S(2)}, u32[]{:S(2)}) collective-permute-start(f32[256,128]{1,0:T(8,128)S(1)} %get-tuple-element.18), channel_id=1, source_target_pairs={{0,1},{1,0},{2,3},{3,2},{4,5},{5,4},{6,7},{7,6},{8,9},{9,8},{10,11... | collective-permute-start | bytes 393224 | tf_op jit(solution)/shard_map/ppermute | solution.py:396
  64.2 1.0 %collective-permute-done.7 = f32[256,128]{1,0:T(8,128)S(1)} collective-permute-done((f32[256,128]{1,0:T(8,128)S(1)}, f32[256,128]{1,0:T(8,128)S(1)}, u32[]{:S(2)}, u32[]{:S(2)}) %collective-permute-start.7) | collective-permute-done | bytes 131104 | tf_op jit(solution)/shard_map/ppermute | solution.py:396
  65.2 0.7 %add.3 = f32[256,128]{1,0:T(8,128)} add(f32[256,128]{1,0:T(8,128)S(1)} %get-tuple-element.17, f32[256,128]{1,0:T(8,128)S(1)} %collective-permute-done.7) | non-fusion elementwise | flops 32768 | bytes 393216 | tf_op jit(solution)/shard_map/add | solution.py:397
  (7 shorter events, 0.1 us)
Async XLA Ops:
  2.6 3.6 %collective-permute-start = (bf16[1,2,64,256]{3,2,1,0:T(8,128)(2,1)S(1)}, bf16[1,2,64,256]{3,2,1,0:T(8,128)(2,1)S(1)}, u32[]{:S(2)}, u32[]{:S(2)}) collective-permute-start(bf16[1,2,64,256]{3,2,1,0:T(8,128)(2,1)S(1)} %bitcast.12), channel_id=1, source_target_pairs={{0,8},{2,10},{4,12},{6,14},{8,0},{10,2},{12,4},{14,6},{16,24},{18,... | collective-permute-start | bytes 196616 | tf_op jit(solution)/shard_map/ppermute | solution.py:270
  2.9 4.1 %collective-permute-start.1 = (bf16[1,2,64,256]{3,2,1,0:T(8,128)(2,1)S(1)}, bf16[1,2,64,256]{3,2,1,0:T(8,128)(2,1)S(1)}, u32[]{:S(2)}, u32[]{:S(2)}) collective-permute-start(bf16[1,2,64,256]{3,2,1,0:T(8,128)(2,1)S(1)} %bitcast.13), channel_id=1, source_target_pairs={{0,16},{2,18},{4,20},{6,22},{8,24},{10,26},{12,28},{14,30},{16,0},... | collective-permute-start | bytes 196616 | tf_op jit(solution)/shard_map/ppermute | solution.py:270
  2.9 5.8 %collective-permute-start.2 = (bf16[1,2,64,256]{3,2,1,0:T(8,128)(2,1)S(1)}, bf16[1,2,64,256]{3,2,1,0:T(8,128)(2,1)S(1)}, u32[]{:S(2)}, u32[]{:S(2)}) collective-permute-start(bf16[1,2,64,256]{3,2,1,0:T(8,128)(2,1)S(1)} %bitcast.14), channel_id=1, source_target_pairs={{0,24},{2,26},{4,28},{6,30},{8,16},{10,18},{12,20},{14,22},{16,8},... | collective-permute-start | bytes 196616 | tf_op jit(solution)/shard_map/ppermute | solution.py:270
  8.8 5.3 %collective-permute-start.3 = (bf16[4,2,64,256]{3,2,1,0:T(8,128)(2,1)S(1)}, bf16[4,2,64,256]{3,2,1,0:T(8,128)(2,1)S(1)}, u32[]{:S(2)}, u32[]{:S(2)}) collective-permute-start(bf16[4,2,64,256]{3,2,1,0:T(8,128)(2,1)S(1)} %bitcast.8), channel_id=1, source_target_pairs={{0,2},{2,0},{4,6},{6,4},{8,10},{10,8},{12,14},{14,12},{16,18},{18,... | collective-permute-start | bytes 786440 | tf_op jit(solution)/shard_map/ppermute | solution.py:270
  9.1 5.2 %collective-permute-start.4 = (bf16[4,2,64,256]{3,2,1,0:T(8,128)(2,1)S(1)}, bf16[4,2,64,256]{3,2,1,0:T(8,128)(2,1)S(1)}, u32[]{:S(2)}, u32[]{:S(2)}) collective-permute-start(bf16[4,2,64,256]{3,2,1,0:T(8,128)(2,1)S(1)} %bitcast.9), channel_id=1, source_target_pairs={{0,4},{2,6},{4,0},{6,2},{8,12},{10,14},{12,8},{14,10},{16,20},{18,... | collective-permute-start | bytes 786440 | tf_op jit(solution)/shard_map/ppermute | solution.py:270
  10.3 9.6 %collective-permute-start.5 = (bf16[4,2,64,256]{3,2,1,0:T(8,128)(2,1)S(1)}, bf16[4,2,64,256]{3,2,1,0:T(8,128)(2,1)S(1)}, u32[]{:S(2)}, u32[]{:S(2)}) collective-permute-start(bf16[4,2,64,256]{3,2,1,0:T(8,128)(2,1)S(1)} %bitcast.10), channel_id=1, source_target_pairs={{0,6},{2,4},{4,2},{6,0},{8,14},{10,12},{12,10},{14,8},{16,22},{18,... | collective-permute-start | bytes 786440 | tf_op jit(solution)/shard_map/ppermute | solution.py:270
  20.0 32.7 %collective-permute-start.6 = (bf16[16,2,64,256]{3,2,1,0:T(8,128)(2,1)S(1)}, bf16[16,2,64,256]{3,2,1,0:T(8,128)(2,1)S(1)}, u32[]{:S(2)}, u32[]{:S(2)}) collective-permute-start(bf16[16,2,64,256]{3,2,1,0:T(8,128)(2,1)S(1)} %bitcast.6), channel_id=1, source_target_pairs={{0,1},{1,0},{2,3},{3,2},{4,5},{5,4},{6,7},{7,6},{8,9},{9,8},{10,11... | collective-permute-start | bytes 3145736 | tf_op jit(solution)/shard_map/ppermute | solution.py:325
  24.3 13.8 %all-to-all-start = ((bf16[16,8,1024]{2,1,0:T(8,128)(2,1)}), bf16[16,8,1024]{2,1,0:T(8,128)(2,1)S(1)}, u32[]{:S(2)}, u32[]{:S(2)}) async-start(bf16[16,8,1024]{2,1,0:T(8,128)(2,1)} %get-tuple-element.12), calls=%async_computation | async-start | bytes 524288 | tf_op jit(solution)/shard_map/all_to_all | solution.py:323
  40.4 17.5 %all-to-all-start.1 = ((bf16[16,8,1024]{2,1,0:T(8,128)(2,1)}), bf16[16,8,1024]{2,1,0:T(8,128)(2,1)S(1)}, u32[]{:S(2)}, u32[]{:S(2)}) async-start(bf16[16,8,1024]{2,1,0:T(8,128)(2,1)} %far.1), calls=%async_computation.1 | async-start | bytes 524288 | tf_op jit(solution)/shard_map/all_to_all | solution.py:360
  46.5 11.5 %copy-start = (bf16[2,512,256]{2,1,0:T(8,128)(2,1)S(1)}, bf16[2,512,256]{2,1,0:T(8,128)(2,1)}, u32[]{:S(2)}) copy-start(bf16[2,512,256]{2,1,0:T(8,128)(2,1)} %dec_ref.1) | copy-start | bytes 1572868
  58.6 6.6 %collective-permute-start.7 = (f32[256,128]{1,0:T(8,128)S(1)}, f32[256,128]{1,0:T(8,128)S(1)}, u32[]{:S(2)}, u32[]{:S(2)}) collective-permute-start(f32[256,128]{1,0:T(8,128)S(1)} %get-tuple-element.18), channel_id=1, source_target_pairs={{0,1},{1,0},{2,3},{3,2},{4,5},{5,4},{6,7},{7,6},{8,9},{9,8},{10,11... | collective-permute-start | bytes 393224 | tf_op jit(solution)/shard_map/ppermute | solution.py:396
where the time goes:
time: 66.3 us; the launch traced here: 65.9 us
  starting transfers between devices  29 us (44%)
  Pallas kernels  19.1 us (29%)
  waiting for transfers between devices  17 us (26%)
  other arithmetic  0.67 us (1%)
    pallas_call x2, Pallas kernels, near(): pl.pallas_call(functools.partial(near_kernel, share, is_mine), out_shape=...  11.4 us
    ppermute x6, waiting for transfers between devices, gather_shares(): lax.ppermute(held, 'box', [(i, i ^ delta * low) for i in range(size)])  10.9 us
    all_to_all x1, starting transfers between devices, whole_product(): lax.all_to_all(coded, 'box', split_axis=0, concat_axis=0, tiled=True)  6.8 us
    ppermute x6, starting transfers between devices, gather_shares(): lax.ppermute(held, 'box', [(i, i ^ delta * low) for i in range(size)])  6.33 us
    all_to_all x1, starting transfers between devices, whole_product(): lax.all_to_all(far, 'box', split_axis=0, concat_axis=0, tiled=True)  6.07 us
    ppermute x1, starting transfers between devices, whole_product(): swapped = lax.ppermute(other, 'dir', [(i, 1 - i) for i in range(sides)])  5.57 us
    all_to_all x1, waiting for transfers between devices, whole_product(): lax.all_to_all(coded, 'box', split_axis=0, concat_axis=0, tiled=True)  5.05 us
    ppermute x1, starting transfers between devices, whole_product(): theirs = lax.ppermute(mine, 'dir', [(i, 1 - i) for i in range(sides)])  4.28 us
  transfers between devices with their start and end apart: 10, of which 7 were waited for; matrix products, arithmetic and copies ran while one was open for 0% of the time, Pallas kernels for 24%

commit v1 on v0

--- a/solution.py
+++ b/solution.py
@@ -81,7 +81,10 @@
                 ).astype(BF16)
 
 
-def table_kernel(grid_x, parts, box_hbm, kern_hbm, cell_hbm, full_hbm, fwd_ref, inv_ref, spec_ref, box_ref, kern_ref, cell_ref, full_ref, sem):
+def table_kernel(
+    grid_x, parts, share, list_ref, mask_ref, box_hbm, kern_hbm, cell_hbm, full_hbm,
+    fwd_ref, inv_ref, spec_ref, order_ref, box_ref, kern_ref, cell_ref, full_ref, sem,
+):
     copies = [
         pltpu.make_async_copy(box_hbm, box_ref, sem.at[0]),
         pltpu.make_async_copy(cell_hbm, cell_ref, sem.at[1]),
@@ -90,6 +93,7 @@
     ]
     for copy in copies:
         copy.start()
+    list_slots(share, list_ref, mask_ref, order_ref)
     full_hi, full_lo = full_ref.at[0], full_ref.at[1]
     cell_hi, cell_lo = cell_ref.at[0], cell_ref.at[1]
     plane = full_hi.shape[0] // 2
@@ -166,51 +170,85 @@
         out_ref[:, :, cols] = total.astype(BF16).reshape(owners, rows, step)
 
 
-def near_kernel(share, mine, list_ref, mask_ref, src_ref, blocks_ref, base_ref, out_ref, blk, acc, sem):
-    boxes, slots = blocks_ref.shape[0], blocks_ref.shape[1]
-    unknowns = blocks_ref.shape[4]
+def list_slots(share, list_ref, mask_ref, order_ref):
+    boxes, slots = list_ref.shape
+    count = boxes * slots
     me, side = lax.axis_index("box"), lax.axis_index("dir")
-    wanted = side if mine else 1 - side
-
-    def used(box, slot):
-        return (mask_ref[box, slot] != 0) & (list_ref[box, slot] % boxes // share == wanted)
-
-    def block_copy(box, slot):
-        n = box * slots + slot
-        return pltpu.make_async_copy(blocks_ref.at[box, slot], blk.at[n], sem.at[n])
-
+    owners = lax.axis_size("box")
     for box in range(boxes):
 
-        @pl.loop(0, slots)
-        def _(slot):
-            @pl.when(used(box, slot))
+        def visit(slot, filled):
+            valid = mask_ref[box, slot] != 0
+
+            @pl.when(valid)
             def _():
-                block_copy(box, slot).start()
-
-    half = src_ref.shape[2] // 2
+                source = list_ref[box, slot]
+                owner, place = lax.div(source, boxes), lax.rem(source, boxes)
+                from_other = (lax.div(place, share) != side).astype(jnp.int32)
+                entry = (from_other * owners + (owner ^ me)) * share + lax.rem(place, share)
+                order_ref[box * slots + filled] = entry
+                order_ref[count + box * slots + filled] = box * slots + slot
+
+            return filled + valid.astype(jnp.int32)
+
+        filled = lax.fori_loop(0, slots, visit, jnp.int32(0))
+        order_ref[2 * count + box] = filled
+
+        @pl.loop(filled, slots)
+        def _(rank):
+            order_ref[box * slots + rank] = 0
+            order_ref[count + box * slots + rank] = count
+
+
+def fetch_kernel(mask_ref, blocks_hbm, blk_ref, sem):
+    boxes, slots = blocks_hbm.shape[0], blocks_hbm.shape[1]
+    count = boxes * slots
+
+    def visit(fn):
+        for box in range(boxes):
+            for slot in range(slots):
+
+                @pl.when(mask_ref[box, slot] != 0)
+                def _():
+                    fn(pltpu.make_async_copy(blocks_hbm.at[box, slot], blk_ref.at[box * slots + slot], sem))
+
+    visit(lambda copy: copy.start())
+    blk_ref[count] = jnp.zeros(blk_ref.shape[1:], BF16)
+    visit(lambda copy: copy.wait())
+
+
+def near_kernel(boxes, order_ref, mine_ref, theirs_ref, blk_ref, out_ref, src, acc):
+    count = blk_ref.shape[0] - 1
+    slots = count // boxes
+    held = mine_ref.shape[0] * mine_ref.shape[1]
+    src[:held] = mine_ref[...].reshape((held,) + mine_ref.shape[2:])
+    src[held:] = theirs_ref[...].reshape((held,) + theirs_ref.shape[2:])
+
+    def product(box, ranks):
+        entries = [box * slots + rank for rank in ranks]
+        vectors = jnp.concatenate([src[order_ref[n]] for n in entries], axis=1)
+        places = [order_ref[count + n] for n in entries]
+        return [
+            dot_nt(vectors, jnp.concatenate([blk_ref[place, part] for place in places], axis=1)) for part in range(2)
+        ]
+
+    first = (slots + 1) // 2 + 1
     for box in range(boxes):
-        acc[...] = jnp.zeros_like(acc)
-
-        @pl.loop(0, slots)
-        def _(slot):
-            @pl.when(used(box, slot))
-            def _():
-                block_copy(box, slot).wait()
-                n = box * slots + slot
-                source = list_ref[box, slot]
-                vector = src_ref[(source // boxes) ^ me, source % share]
-                acc[...] += jnp.concatenate([dot_nt(vector, blk[n, 0]), dot_nt(vector, blk[n, 1])], axis=1)
-
-        re, im = slice(0, half), slice(half, 2 * half)
-        with_re, with_im = acc[:, :unknowns], acc[:, unknowns:]
-        near_re = with_re[re] - with_im[im]
-        near_im = with_re[im] + with_im[re]
+        acc[box, 0], acc[box, 1] = product(box, range(first))
+    for box in range(boxes):
+
+        @pl.when(order_ref[2 * count + box] > first)
+        def _():
+            more = product(box, range(first, slots))
+            acc[box, 0] += more[0]
+            acc[box, 1] += more[1]
+
+    half = src.shape[1] // 2
+    re, im = slice(0, half), slice(half, 2 * half)
+    for box in range(boxes):
         rows_re, rows_im = part_rows(box, half)
-        if not mine:
-            near_re = near_re + base_ref[rows_re, :]
-            near_im = near_im + base_ref[rows_im, :]
-        out_ref[rows_re, :] = near_re
-        out_ref[rows_im, :] = near_im
+        out_ref[rows_re, :] = acc[box, 0, re, :] - acc[box, 1, im, :]
+        out_ref[rows_im, :] = acc[box, 0, im, :] + acc[box, 1, re, :]
 
 
 def decode_kernel(rhs, group, far_ref, dec_ref, near_ref, own_ref, other_ref, wide, total):
@@ -329,15 +367,17 @@
     point = np.arange(plane)
     full_hi, full_lo = plane_table(point // (2 * GZ), point % (2 * GZ))
     constants = (np.stack([cell_hi, cell_lo]), np.stack([full_hi, full_lo]))
-    forward, inverse, spectrum = pl.pallas_call(
-        functools.partial(table_kernel, grid_x, parts),
+    count = per_box * near_list.shape[1]
+    forward, inverse, spectrum, order = pl.pallas_call(
+        functools.partial(table_kernel, grid_x, parts, share),
         out_shape=(
             pltpu.VMEM((grid_x, 2 * plane, 2 * parts * boxes), BF16),
             pltpu.VMEM((grid_x, 2, parts * boxes, 2 * plane), BF16),
             pltpu.VMEM((double_x, 2 * plane, LANES), F32),
+            jax.ShapeDtypeStruct((2 * count + per_box,), jnp.int32),
         ),
-        in_specs=[hbm()] * 4,
-        out_specs=(vmem(),) * 3,
+        in_specs=[smem(), smem()] + [hbm()] * 4,
+        out_specs=(vmem(), vmem(), vmem(), smem()),
         scratch_shapes=[
             pltpu.VMEM((1, boxes), jnp.int32),
             pltpu.VMEM(kernel.shape, F32),
@@ -347,7 +387,7 @@
         ],
         compiler_params=budget(24),
         name="tables",
-    )(stay(box_cell[None, :]), stay(kernel), *[stay(jnp.asarray(table)) for table in constants])
+    )(stay(near_list), stay(near_mask), stay(box_cell[None, :]), stay(kernel), *[stay(jnp.asarray(table)) for table in constants])
 
     far = pl.pallas_call(
         functools.partial(far_kernel, grid_x),
@@ -360,25 +400,27 @@
     returned = lax.all_to_all(far, "box", split_axis=0, concat_axis=0, tiled=True)
 
 
-    slots = near_list.shape[1]
-
-    def near(is_mine, vectors, base):
-        return pl.pallas_call(
-            functools.partial(near_kernel, share, is_mine),
-            out_shape=pltpu.VMEM((rows * rhs, unknowns), F32),
-            in_specs=[smem(), smem(), vmem(), hbm(), vmem()],
-            out_specs=vmem(),
-            scratch_shapes=[
-                pltpu.VMEM((per_box * slots, parts, unknowns, unknowns), BF16),
-                pltpu.VMEM((parts * rhs, parts * unknowns), F32),
-                pltpu.SemaphoreType.DMA((per_box * slots,)),
-            ],
-            compiler_params=budget(20),
-            name="near_mine" if is_mine else "near_theirs",
-        )(stay(near_list), stay(near_mask), vectors, stay(near_blocks), base)
-
-    near_part = near(True, mine, own_share)
-    near_part = near(False, theirs, near_part)
+    blocks = pl.pallas_call(
+        fetch_kernel,
+        out_shape=pltpu.VMEM((count + 1,) + near_blocks.shape[2:], BF16),
+        in_specs=[smem(), hbm()],
+        out_specs=vmem(),
+        scratch_shapes=[pltpu.SemaphoreType.DMA],
+        compiler_params=budget(4),
+        name="fetch",
+    )(stay(near_mask), stay(near_blocks))
+    near_part = pl.pallas_call(
+        functools.partial(near_kernel, per_box),
+        out_shape=pltpu.VMEM((rows * rhs, unknowns), F32),
+        in_specs=[smem(), vmem(), vmem(), vmem()],
+        out_specs=vmem(),
+        scratch_shapes=[
+            pltpu.VMEM((sides * owners * share, parts * rhs, unknowns), BF16),
+            pltpu.VMEM((per_box, parts, parts * rhs, unknowns), F32),
+        ],
+        compiler_params=budget(12),
+        name="near",
+    )(order, mine, theirs, blocks)
 
     half = unknowns // sides
     own, other = pl.pallas_call(

time: 66.3 us -> 61.4 us (0.926)
  the two profiles are of different devices: /device:TPU:27 before, /device:TPU:0 now
where the time goes in v1:
time: 61.4 us; the launch traced here: 61 us
  waiting for transfers between devices  27.7 us (45%)
  starting transfers between devices  17 us (28%)
  Pallas kernels  15.5 us (25%)
  other arithmetic  0.67 us (1%)
    ppermute x6, waiting for transfers between devices, gather_shares(): lax.ppermute(held, 'box', [(i, i ^ delta * low) for i in range(size)])  16.1 us
    ppermute x6, starting transfers between devices, gather_shares(): lax.ppermute(held, 'box', [(i, i ^ delta * low) for i in range(size)])  9.34 us
    all_to_all x1, waiting for transfers between devices, whole_product(): lax.all_to_all(coded, 'box', split_axis=0, concat_axis=0, tiled=True)  7.26 us
    all_to_all x1, starting transfers between devices, whole_product(): lax.all_to_all(coded, 'box', split_axis=0, concat_axis=0, tiled=True)  3.97 us
    all_to_all x1, starting transfers between devices, whole_product(): lax.all_to_all(far, 'box', split_axis=0, concat_axis=0, tiled=True)  3.55 us
    pallas_call x1, Pallas kernels, whole_product(): pl.pallas_call(functools.partial(near_kernel, per_box), out_shape=pltpu.V...  3.31 us
    pallas_call x1, Pallas kernels, whole_product(): pl.pallas_call(functools.partial(table_kernel, grid_x, parts, share), out...  3.26 us
    pallas_call x1, Pallas kernels, whole_product(): pl.pallas_call(fetch_kernel, out_shape=pltpu.VMEM((count + 1,) + near_blo...  3.17 us
  transfers between devices with their start and end apart: 10, of which 8 were waited for; matrix products, arithmetic and copies ran while one was open for 0% of the time, Pallas kernels for 20%

profile of v1, /device:TPU:0, one launch (start us, length us, event | category | flops | bytes accessed | tf_op | source)
XLA Modules:
  0.0 61.0 jit_solution(31835943465916991)
XLA Ops:
  0.0 2.6 %encode.1 = (bf16[16,8,1024]{2,1,0:T(8,128)(2,1)}, bf16[128,256]{1,0:T(8,128)(2,1)S(1)}) custom-call(bf16[256,256]{1,0:T(8,128)(2,1)} %bitcast.16, bf16[2,512,256]{2,1,0:T(8,128)(2,1)} %enc_hbm.1), custom_call_target="tpu_custom_call" | custom-call | tf_op jit(solution)/shard_map/encode/pallas_call | solution.py:344
  2.6 5.1 %collective-permute-start.2 = (bf16[1,2,64,256]{3,2,1,0:T(8,128)(2,1)S(1)}, bf16[1,2,64,256]{3,2,1,0:T(8,128)(2,1)S(1)}, u32[]{:S(2)}, u32[]{:S(2)}) collective-permute-start(bf16[1,2,64,256]{3,2,1,0:T(8,128)(2,1)S(1)} %bitcast.12), channel_id=1, source_target_pairs={{0,24},{2,26},{4,28},{6,30},{8,16},{10,18},{12,20},{14,22},{16,8},... | collective-permute-start | bytes 196616 | tf_op jit(solution)/shard_map/ppermute | solution.py:308
  7.8 0.6 %collective-permute-start = (bf16[1,2,64,256]{3,2,1,0:T(8,128)(2,1)S(1)}, bf16[1,2,64,256]{3,2,1,0:T(8,128)(2,1)S(1)}, u32[]{:S(2)}, u32[]{:S(2)}) collective-permute-start(bf16[1,2,64,256]{3,2,1,0:T(8,128)(2,1)S(1)} %bitcast.14), channel_id=1, source_target_pairs={{0,8},{2,10},{4,12},{6,14},{8,0},{10,2},{12,4},{14,6},{16,24},{18,... | collective-permute-start | bytes 196616 | tf_op jit(solution)/shard_map/ppermute | solution.py:308
  8.4 1.8 %collective-permute-done.2.refs_3_ = bf16[1,2,64,256]{3,2,1,0:T(8,128)(2,1)S(1)} collective-permute-done((bf16[1,2,64,256]{3,2,1,0:T(8,128)(2,1)S(1)}, bf16[1,2,64,256]{3,2,1,0:T(8,128)(2,1)S(1)}, u32[]{:S(2)}, u32[]{:S(2)}) %collective-permute-start.2) | collective-permute-done | bytes 65568 | tf_op jit(solution)/shard_map/ppermute | solution.py:308
  10.3 3.1 %collective-permute-done.1.refs_2_ = bf16[1,2,64,256]{3,2,1,0:T(8,128)(2,1)S(1)} collective-permute-done((bf16[1,2,64,256]{3,2,1,0:T(8,128)(2,1)S(1)}, bf16[1,2,64,256]{3,2,1,0:T(8,128)(2,1)S(1)}, u32[]{:S(2)}, u32[]{:S(2)}) %collective-permute-start.1) | collective-permute-done | bytes 65568 | tf_op jit(solution)/shard_map/ppermute | solution.py:308
  13.4 2.5 %collective-permute-start.5 = (bf16[4,2,64,256]{3,2,1,0:T(8,128)(2,1)S(1)}, bf16[4,2,64,256]{3,2,1,0:T(8,128)(2,1)S(1)}, u32[]{:S(2)}, u32[]{:S(2)}) collective-permute-start(bf16[4,2,64,256]{3,2,1,0:T(8,128)(2,1)S(1)} %bitcast.8), channel_id=1, source_target_pairs={{0,6},{2,4},{4,2},{6,0},{8,14},{10,12},{12,10},{14,8},{16,22},{18,... | collective-permute-start | bytes 786440 | tf_op jit(solution)/shard_map/ppermute | solution.py:308
  15.9 0.5 collective-permute-start.4
  16.4 0.5 collective-permute-start.3
  17.0 6.6 %collective-permute-done.5.refs_3_ = bf16[4,2,64,256]{3,2,1,0:T(8,128)(2,1)S(1)} collective-permute-done((bf16[4,2,64,256]{3,2,1,0:T(8,128)(2,1)S(1)}, bf16[4,2,64,256]{3,2,1,0:T(8,128)(2,1)S(1)}, u32[]{:S(2)}, u32[]{:S(2)}) %collective-permute-start.5) | collective-permute-done | bytes 262176 | tf_op jit(solution)/shard_map/ppermute | solution.py:308
  23.6 4.3 %collective-permute-done.4.refs_2_ = bf16[4,2,64,256]{3,2,1,0:T(8,128)(2,1)S(1)} collective-permute-done((bf16[4,2,64,256]{3,2,1,0:T(8,128)(2,1)S(1)}, bf16[4,2,64,256]{3,2,1,0:T(8,128)(2,1)S(1)}, u32[]{:S(2)}, u32[]{:S(2)}) %collective-permute-start.4) | collective-permute-done | bytes 262176 | tf_op jit(solution)/shard_map/ppermute | solution.py:308
  27.9 0.2 collective-permute-done.3.refs_1_
  28.2 0.1 collective-permute-start.6
  28.2 4.0 %all-to-all-start = ((bf16[16,8,1024]{2,1,0:T(8,128)(2,1)}), bf16[16,8,1024]{2,1,0:T(8,128)(2,1)S(1)}, u32[]{:S(2)}, u32[]{:S(2)}) async-start(bf16[16,8,1024]{2,1,0:T(8,128)(2,1)} %get-tuple-element.13), calls=%async_computation | async-start | bytes 524288 | tf_op jit(solution)/shard_map/all_to_all | solution.py:361
  32.2 3.3 %tables.1 = (bf16[2,256,256]{2,1,0:T(8,128)(2,1)S(1)}, bf16[2,2,128,256]{3,2,1,0:T(8,128)(2,1)S(1)}, f32[4,256,128]{2,1,0:T(8,128)S(1)}, s32[116]{0:T(128)S(1)}) custom-call(s32[4,14]{1,0:T(4,128)} %list_ref.1, s32[4,14]{1,0:T(4,128)} %mask_ref.3, s32[1,64]{1,0:T(1,128)} %bitcast.17, f32[32,2,4,128]{3,2,1,0:T(4,128)} %kern_hbm.1, ...), custom_call_target="tpu_custom_call" | custom-call | tf_op jit(solution)/shard_map/tables/pallas_call | solution.py:371
  35.5 7.3 %all-to-all-done.coded_ref = bf16[16,8,1024]{2,1,0:T(8,128)(2,1)S(1)} async-done(((bf16[16,8,1024]{2,1,0:T(8,128)(2,1)}), bf16[16,8,1024]{2,1,0:T(8,128)(2,1)S(1)}, u32[]{:S(2)}, u32[]{:S(2)}) %all-to-all-start) | async-done | bytes 262176 | tf_op jit(solution)/shard_map/all_to_all | solution.py:361
  42.7 2.4 %far.1 = bf16[16,8,1024]{2,1,0:T(8,128)(2,1)} custom-call(bf16[16,8,1024]{2,1,0:T(8,128)(2,1)S(1)} %all-to-all-done.coded_ref, bf16[2,256,256]{2,1,0:T(8,128)(2,1)S(1)} %get-tuple-element.14.fwd_ref, bf16[2,2,128,256]{3,2,1,0:T(8,128)(2,1)S(1)} %get-tuple-element.15.inv_ref, f32[4,256,128]{2,1,0:T(8,128)S(1)} %get-tuple-element.16.spec_ref), custom_call_target="tpu_custom_call" | custom-call | tf_op jit(solution)/shard_map/far/pallas_call | solution.py:392
  45.1 3.5 %all-to-all-start.1 = ((bf16[16,8,1024]{2,1,0:T(8,128)(2,1)}), bf16[16,8,1024]{2,1,0:T(8,128)(2,1)S(1)}, u32[]{:S(2)}, u32[]{:S(2)}) async-start(bf16[16,8,1024]{2,1,0:T(8,128)(2,1)} %far.1), calls=%async_computation.1 | async-start | bytes 524288 | tf_op jit(solution)/shard_map/all_to_all | solution.py:400
  48.7 3.2 %fetch.1.blk_ref = bf16[57,2,256,256]{3,2,1,0:T(8,128)(2,1)S(1)} custom-call(s32[4,14]{1,0:T(4,128)} %mask_ref.3, bf16[4,14,2,256,256]{4,3,2,1,0:T(8,128)(2,1)} %blocks_hbm.1), custom_call_target="tpu_custom_call" | custom-call | tf_op jit(solution)/shard_map/fetch/pallas_call | solution.py:403
  51.9 3.3 %near.1.near_ref = f32[256,256]{1,0:T(8,128)S(1)} custom-call(s32[116]{0:T(128)S(1)} %get-tuple-element.17.order_ref, bf16[16,2,64,256]{3,2,1,0:T(8,128)(2,1)S(1)} %bitcast.7, bf16[16,2,64,256]{3,2,1,0:T(8,128)(2,1)S(1)} %collective-permute-done.6.theirs_ref, bf16[57,2,256,256]{3,2,1,0:T(8,128)(2,1)S(1)} %fetch.1.blk_ref), custom_call_target="tpu_custom_call" | custom-call | tf_op jit(solution)/shard_map/near/pallas_call | solution.py:412
  55.2 3.0 %all-to-all-done.1.far_ref = bf16[16,8,1024]{2,1,0:T(8,128)(2,1)S(1)} async-done(((bf16[16,8,1024]{2,1,0:T(8,128)(2,1)}), bf16[16,8,1024]{2,1,0:T(8,128)(2,1)S(1)}, u32[]{:S(2)}, u32[]{:S(2)}) %all-to-all-start.1) | async-done | bytes 262176 | tf_op jit(solution)/shard_map/all_to_all | solution.py:400
  58.2 0.7 %decode.1 = (f32[256,128]{1,0:T(8,128)S(1)}, f32[256,128]{1,0:T(8,128)S(1)}) custom-call(bf16[16,8,1024]{2,1,0:T(8,128)(2,1)S(1)} %all-to-all-done.1.far_ref, bf16[2,512,256]{2,1,0:T(8,128)(2,1)S(1)} %copy-done, f32[256,256]{1,0:T(8,128)S(1)} %near.1.near_ref), custom_call_target="tpu_custom_call" | custom-call | tf_op jit(solution)/shard_map/decode/pallas_call | solution.py:426
  58.9 0.1 collective-permute-start.7
  58.9 1.3 %collective-permute-done.7 = f32[256,128]{1,0:T(8,128)S(1)} collective-permute-done((f32[256,128]{1,0:T(8,128)S(1)}, f32[256,128]{1,0:T(8,128)S(1)}, u32[]{:S(2)}, u32[]{:S(2)}) %collective-permute-start.7) | collective-permute-done | bytes 131104 | tf_op jit(solution)/shard_map/ppermute | solution.py:438
  60.3 0.7 %add.3 = f32[256,128]{1,0:T(8,128)} add(f32[256,128]{1,0:T(8,128)S(1)} %get-tuple-element.19, f32[256,128]{1,0:T(8,128)S(1)} %collective-permute-done.7) | non-fusion elementwise | flops 32768 | bytes 393216 | tf_op jit(solution)/shard_map/add | solution.py:439
  (7 shorter events, 0.1 us)
Async XLA Ops:
  2.6 7.6 %collective-permute-start.2 = (bf16[1,2,64,256]{3,2,1,0:T(8,128)(2,1)S(1)}, bf16[1,2,64,256]{3,2,1,0:T(8,128)(2,1)S(1)}, u32[]{:S(2)}, u32[]{:S(2)}) collective-permute-start(bf16[1,2,64,256]{3,2,1,0:T(8,128)(2,1)S(1)} %bitcast.12), channel_id=1, source_target_pairs={{0,24},{2,26},{4,28},{6,30},{8,16},{10,18},{12,20},{14,22},{16,8},... | collective-permute-start | bytes 196616 | tf_op jit(solution)/shard_map/ppermute | solution.py:308
  7.8 5.6 %collective-permute-start.1 = (bf16[1,2,64,256]{3,2,1,0:T(8,128)(2,1)S(1)}, bf16[1,2,64,256]{3,2,1,0:T(8,128)(2,1)S(1)}, u32[]{:S(2)}, u32[]{:S(2)}) collective-permute-start(bf16[1,2,64,256]{3,2,1,0:T(8,128)(2,1)S(1)} %bitcast.13), channel_id=1, source_target_pairs={{0,16},{2,18},{4,20},{6,22},{8,24},{10,26},{12,28},{14,30},{16,0},... | collective-permute-start | bytes 196616 | tf_op jit(solution)/shard_map/ppermute | solution.py:308
  7.8 5.6 %collective-permute-start = (bf16[1,2,64,256]{3,2,1,0:T(8,128)(2,1)S(1)}, bf16[1,2,64,256]{3,2,1,0:T(8,128)(2,1)S(1)}, u32[]{:S(2)}, u32[]{:S(2)}) collective-permute-start(bf16[1,2,64,256]{3,2,1,0:T(8,128)(2,1)S(1)} %bitcast.14), channel_id=1, source_target_pairs={{0,8},{2,10},{4,12},{6,14},{8,0},{10,2},{12,4},{14,6},{16,24},{18,... | collective-permute-start | bytes 196616 | tf_op jit(solution)/shard_map/ppermute | solution.py:308
  13.4 10.2 %collective-permute-start.5 = (bf16[4,2,64,256]{3,2,1,0:T(8,128)(2,1)S(1)}, bf16[4,2,64,256]{3,2,1,0:T(8,128)(2,1)S(1)}, u32[]{:S(2)}, u32[]{:S(2)}) collective-permute-start(bf16[4,2,64,256]{3,2,1,0:T(8,128)(2,1)S(1)} %bitcast.8), channel_id=1, source_target_pairs={{0,6},{2,4},{4,2},{6,0},{8,14},{10,12},{12,10},{14,8},{16,22},{18,... | collective-permute-start | bytes 786440 | tf_op jit(solution)/shard_map/ppermute | solution.py:308
  15.9 11.9 %collective-permute-start.4 = (bf16[4,2,64,256]{3,2,1,0:T(8,128)(2,1)S(1)}, bf16[4,2,64,256]{3,2,1,0:T(8,128)(2,1)S(1)}, u32[]{:S(2)}, u32[]{:S(2)}) collective-permute-start(bf16[4,2,64,256]{3,2,1,0:T(8,128)(2,1)S(1)} %bitcast.9), channel_id=1, source_target_pairs={{0,4},{2,6},{4,0},{6,2},{8,12},{10,14},{12,8},{14,10},{16,20},{18,... | collective-permute-start | bytes 786440 | tf_op jit(solution)/shard_map/ppermute | solution.py:308
  16.4 11.7 %collective-permute-start.3 = (bf16[4,2,64,256]{3,2,1,0:T(8,128)(2,1)S(1)}, bf16[4,2,64,256]{3,2,1,0:T(8,128)(2,1)S(1)}, u32[]{:S(2)}, u32[]{:S(2)}) collective-permute-start(bf16[4,2,64,256]{3,2,1,0:T(8,128)(2,1)S(1)} %bitcast.10), channel_id=1, source_target_pairs={{0,2},{2,0},{4,6},{6,4},{8,10},{10,8},{12,14},{14,12},{16,18},{18,... | collective-permute-start | bytes 786440 | tf_op jit(solution)/shard_map/ppermute | solution.py:308
  28.2 23.7 %collective-permute-start.6 = (bf16[16,2,64,256]{3,2,1,0:T(8,128)(2,1)S(1)}, bf16[16,2,64,256]{3,2,1,0:T(8,128)(2,1)S(1)}, u32[]{:S(2)}, u32[]{:S(2)}) collective-permute-start(bf16[16,2,64,256]{3,2,1,0:T(8,128)(2,1)S(1)} %bitcast.6), channel_id=1, source_target_pairs={{0,1},{1,0},{2,3},{3,2},{4,5},{5,4},{6,7},{7,6},{8,9},{9,8},{10,11... | collective-permute-start | bytes 3145736 | tf_op jit(solution)/shard_map/ppermute | solution.py:363
  28.2 14.5 %all-to-all-start = ((bf16[16,8,1024]{2,1,0:T(8,128)(2,1)}), bf16[16,8,1024]{2,1,0:T(8,128)(2,1)S(1)}, u32[]{:S(2)}, u32[]{:S(2)}) async-start(bf16[16,8,1024]{2,1,0:T(8,128)(2,1)} %get-tuple-element.13), calls=%async_computation | async-start | bytes 524288 | tf_op jit(solution)/shard_map/all_to_all | solution.py:361
  45.1 13.0 %all-to-all-start.1 = ((bf16[16,8,1024]{2,1,0:T(8,128)(2,1)}), bf16[16,8,1024]{2,1,0:T(8,128)(2,1)S(1)}, u32[]{:S(2)}, u32[]{:S(2)}) async-start(bf16[16,8,1024]{2,1,0:T(8,128)(2,1)} %far.1), calls=%async_computation.1 | async-start | bytes 524288 | tf_op jit(solution)/shard_map/all_to_all | solution.py:400
  51.9 6.3 %copy-start = (bf16[2,512,256]{2,1,0:T(8,128)(2,1)S(1)}, bf16[2,512,256]{2,1,0:T(8,128)(2,1)}, u32[]{:S(2)}) copy-start(bf16[2,512,256]{2,1,0:T(8,128)(2,1)} %dec_ref.1) | copy-start | bytes 1572868
  58.9 1.4 %collective-permute-start.7 = (f32[256,128]{1,0:T(8,128)S(1)}, f32[256,128]{1,0:T(8,128)S(1)}, u32[]{:S(2)}, u32[]{:S(2)}) collective-permute-start(f32[256,128]{1,0:T(8,128)S(1)} %get-tuple-element.20), channel_id=1, source_target_pairs={{0,1},{1,0},{2,3},{3,2},{4,5},{5,4},{6,7},{7,6},{8,9},{9,8},{10,11... | collective-permute-start | bytes 393224 | tf_op jit(solution)/shard_map/ppermute | solution.py:438

commit v2 on v1

--- a/solution.py
+++ b/solution.py
@@ -174,81 +174,104 @@
     boxes, slots = list_ref.shape
     count = boxes * slots
     me, side = lax.axis_index("box"), lax.axis_index("dir")
-    owners = lax.axis_size("box")
     for box in range(boxes):
 
         def visit(slot, filled):
             valid = mask_ref[box, slot] != 0
+            source = list_ref[box, slot]
+            owner, place = lax.div(source, boxes), lax.rem(source, boxes)
+            other = lax.div(place, share) != side
+            rank = box * slots + jnp.where(other, filled[1] + count, filled[0])
 
             @pl.when(valid)
             def _():
-                source = list_ref[box, slot]
-                owner, place = lax.div(source, boxes), lax.rem(source, boxes)
-                from_other = (lax.div(place, share) != side).astype(jnp.int32)
-                entry = (from_other * owners + (owner ^ me)) * share + lax.rem(place, share)
-                order_ref[box * slots + filled] = entry
-                order_ref[count + box * slots + filled] = box * slots + slot
-
-            return filled + valid.astype(jnp.int32)
-
-        filled = lax.fori_loop(0, slots, visit, jnp.int32(0))
-        order_ref[2 * count + box] = filled
-
-        @pl.loop(filled, slots)
-        def _(rank):
-            order_ref[box * slots + rank] = 0
-            order_ref[count + box * slots + rank] = count
-
-
-def fetch_kernel(mask_ref, blocks_hbm, blk_ref, sem):
-    boxes, slots = blocks_hbm.shape[0], blocks_hbm.shape[1]
-    count = boxes * slots
-
-    def visit(fn):
-        for box in range(boxes):
-            for slot in range(slots):
-
-                @pl.when(mask_ref[box, slot] != 0)
-                def _():
-                    fn(pltpu.make_async_copy(blocks_hbm.at[box, slot], blk_ref.at[box * slots + slot], sem))
-
-    visit(lambda copy: copy.start())
-    blk_ref[count] = jnp.zeros(blk_ref.shape[1:], BF16)
-    visit(lambda copy: copy.wait())
-
-
-def near_kernel(boxes, order_ref, mine_ref, theirs_ref, blk_ref, out_ref, src, acc):
+                order_ref[rank] = (owner ^ me) * share + lax.rem(place, share)
+                order_ref[2 * count + rank] = box * slots + slot
+
+            return (
+                filled[0] + (valid & ~other).astype(jnp.int32),
+                filled[1] + (valid & other).astype(jnp.int32),
+            )
+
+        filled = lax.fori_loop(0, slots, visit, (jnp.int32(0), jnp.int32(0)))
+        for half in range(2):
+            order_ref[4 * count + half * boxes + box] = filled[half]
+
+            @pl.loop(filled[half], slots)
+            def _(rank):
+                order_ref[half * count + box * slots + rank] = 0
+                order_ref[(2 + half) * count + box * slots + rank] = count
+
+
+def near_products(half, boxes, order_ref, src_ref, blk_ref, acc, arrived):
     count = blk_ref.shape[0] - 1
     slots = count // boxes
-    held = mine_ref.shape[0] * mine_ref.shape[1]
-    src[:held] = mine_ref[...].reshape((held,) + mine_ref.shape[2:])
-    src[held:] = theirs_ref[...].reshape((held,) + theirs_ref.shape[2:])
 
     def product(box, ranks):
-        entries = [box * slots + rank for rank in ranks]
-        vectors = jnp.concatenate([src[order_ref[n]] for n in entries], axis=1)
-        places = [order_ref[count + n] for n in entries]
+        entries = [half * count + box * slots + rank for rank in ranks]
+        places = [order_ref[2 * count + n] for n in entries]
+        sources = [order_ref[n] for n in entries]
+        vectors = jnp.concatenate([src_ref[lax.div(n, src_ref.shape[1]), lax.rem(n, src_ref.shape[1])] for n in sources], axis=1)
         return [
             dot_nt(vectors, jnp.concatenate([blk_ref[place, part] for place in places], axis=1)) for part in range(2)
         ]
 
-    first = (slots + 1) // 2 + 1
-    for box in range(boxes):
+    first = min(6, slots)
+    for box in range(boxes):
+        arrived(box)
         acc[box, 0], acc[box, 1] = product(box, range(first))
     for box in range(boxes):
 
-        @pl.when(order_ref[2 * count + box] > first)
+        @pl.when(order_ref[4 * count + half * boxes + box] > first)
         def _():
             more = product(box, range(first, slots))
             acc[box, 0] += more[0]
             acc[box, 1] += more[1]
 
-    half = src.shape[1] // 2
-    re, im = slice(0, half), slice(half, 2 * half)
-    for box in range(boxes):
-        rows_re, rows_im = part_rows(box, half)
+
+def near_mine_kernel(boxes, order_ref, src_ref, blocks_hbm, blk_ref, out_ref, acc, sem):
+    count = blk_ref.shape[0] - 1
+    slots = count // boxes
+
+    def block_copy(half, box, rank):
+        place = order_ref[(2 + half) * count + box * slots + rank]
+        return pltpu.make_async_copy(
+            blocks_hbm.at[box, place - box * slots], blk_ref.at[place], sem.at[half * boxes + box]
+        )
+
+    for half in range(2):
+        for box in range(boxes):
+
+            @pl.loop(0, order_ref[4 * count + half * boxes + box])
+            def _(rank):
+                block_copy(half, box, rank).start()
+
+    blk_ref[count] = jnp.zeros(blk_ref.shape[1:], BF16)
+
+    def arrived(half, box):
+        @pl.loop(0, order_ref[4 * count + half * boxes + box])
+        def _(rank):
+            block_copy(half, box, rank).wait()
+
+    near_products(0, boxes, order_ref, src_ref, blk_ref, acc, functools.partial(arrived, 0))
+    for box in range(boxes):
+        rows_re, rows_im, re, im = near_rows(box, acc.shape[2] // 2)
         out_ref[rows_re, :] = acc[box, 0, re, :] - acc[box, 1, im, :]
         out_ref[rows_im, :] = acc[box, 0, im, :] + acc[box, 1, re, :]
+    for box in range(boxes):
+        arrived(1, box)
+
+
+def near_theirs_kernel(boxes, order_ref, src_ref, blk_ref, base_ref, out_ref, acc):
+    near_products(1, boxes, order_ref, src_ref, blk_ref, acc, lambda box: None)
+    for box in range(boxes):
+        rows_re, rows_im, re, im = near_rows(box, acc.shape[2] // 2)
+        out_ref[rows_re, :] = base_ref[rows_re, :] + (acc[box, 0, re, :] - acc[box, 1, im, :])
+        out_ref[rows_im, :] = base_ref[rows_im, :] + (acc[box, 0, im, :] + acc[box, 1, re, :])
+
+
+def near_rows(box, half):
+    return (*part_rows(box, half), slice(0, half), slice(half, 2 * half))
 
 
 def decode_kernel(rhs, group, far_ref, dec_ref, near_ref, own_ref, other_ref, wide, total):
@@ -374,7 +397,7 @@
             pltpu.VMEM((grid_x, 2 * plane, 2 * parts * boxes), BF16),
             pltpu.VMEM((grid_x, 2, parts * boxes, 2 * plane), BF16),
             pltpu.VMEM((double_x, 2 * plane, LANES), F32),
-            jax.ShapeDtypeStruct((2 * count + per_box,), jnp.int32),
+            jax.ShapeDtypeStruct((4 * count + 2 * per_box,), jnp.int32),
         ),
         in_specs=[smem(), smem()] + [hbm()] * 4,
         out_specs=(vmem(), vmem(), vmem(), smem()),
@@ -400,27 +423,28 @@
     returned = lax.all_to_all(far, "box", split_axis=0, concat_axis=0, tiled=True)
 
 
-    blocks = pl.pallas_call(
-        fetch_kernel,
-        out_shape=pltpu.VMEM((count + 1,) + near_blocks.shape[2:], BF16),
-        in_specs=[smem(), hbm()],
-        out_specs=vmem(),
-        scratch_shapes=[pltpu.SemaphoreType.DMA],
+    near_acc = pltpu.VMEM((per_box, parts, parts * rhs, unknowns), F32)
+    blocks, near_part = pl.pallas_call(
+        functools.partial(near_mine_kernel, per_box),
+        out_shape=(
+            pltpu.VMEM((count + 1,) + near_blocks.shape[2:], BF16),
+            pltpu.VMEM((rows * rhs, unknowns), F32),
+        ),
+        in_specs=[smem(), vmem(), hbm()],
+        out_specs=(vmem(),) * 2,
+        scratch_shapes=[near_acc, pltpu.SemaphoreType.DMA((2 * per_box,))],
         compiler_params=budget(4),
-        name="fetch",
-    )(stay(near_mask), stay(near_blocks))
+        name="near_mine",
+    )(order, mine, stay(near_blocks))
     near_part = pl.pallas_call(
-        functools.partial(near_kernel, per_box),
+        functools.partial(near_theirs_kernel, per_box),
         out_shape=pltpu.VMEM((rows * rhs, unknowns), F32),
         in_specs=[smem(), vmem(), vmem(), vmem()],
         out_specs=vmem(),
-        scratch_shapes=[
-            pltpu.VMEM((sides * owners * share, parts * rhs, unknowns), BF16),
-            pltpu.VMEM((per_box, parts, parts * rhs, unknowns), F32),
-        ],
-        compiler_params=budget(12),
-        name="near",
-    )(order, mine, theirs, blocks)
+        scratch_shapes=[near_acc],
+        compiler_params=budget(4),
+        name="near_theirs",
+    )(order, theirs, blocks, near_part)
 
     half = unknowns // sides
     own, other = pl.pallas_call(

time: 61.4 us -> 61.3 us (level)
  transfers between devices with their start and end apart: 10 -> 10, of which waited for: 8 -> 8; matrix products, arithmetic and copies ran while one was open for 0% -> 0% of each run, Pallas kernels for 20% -> 21%
where the time goes in v2:
time: 61.3 us; the launch traced here: 60.9 us
  waiting for transfers between devices  27.1 us (44%)
  starting transfers between devices  17 us (28%)
  Pallas kernels  16.1 us (26%)
  other arithmetic  0.67 us (1%)
    ppermute x6, waiting for transfers between devices, gather_shares(): lax.ppermute(held, 'box', [(i, i ^ delta * low) for i in range(size)])  16.1 us
    ppermute x6, starting transfers between devices, gather_shares(): lax.ppermute(held, 'box', [(i, i ^ delta * low) for i in range(size)])  9.34 us
    all_to_all x1, waiting for transfers between devices, whole_product(): lax.all_to_all(coded, 'box', split_axis=0, concat_axis=0, tiled=True)  7.01 us
    pallas_call x1, Pallas kernels, whole_product(): pl.pallas_call(functools.partial(near_mine_kernel, per_box), out_shape=(p...  4.18 us
    all_to_all x1, starting transfers between devices, whole_product(): lax.all_to_all(coded, 'box', split_axis=0, concat_axis=0, tiled=True)  3.97 us
    all_to_all x1, starting transfers between devices, whole_product(): lax.all_to_all(far, 'box', split_axis=0, concat_axis=0, tiled=True)  3.55 us
    pallas_call x1, Pallas kernels, whole_product(): pl.pallas_call(functools.partial(table_kernel, grid_x, parts, share), out...  3.5 us
    all_to_all x1, waiting for transfers between devices, whole_product(): lax.all_to_all(far, 'box', split_axis=0, concat_axis=0, tiled=True)  2.67 us
  transfers between devices with their start and end apart: 10, of which 8 were waited for; matrix products, arithmetic and copies ran while one was open for 0% of the time, Pallas kernels for 21%

profile of v2, /device:TPU:0, one launch (start us, length us, event | category | flops | bytes accessed | tf_op | source)
XLA Modules:
  0.0 60.9 jit_solution(7666472939038789504)
XLA Ops:
  0.0 2.6 %encode.1 = (bf16[16,8,1024]{2,1,0:T(8,128)(2,1)}, bf16[128,256]{1,0:T(8,128)(2,1)S(1)}) custom-call(bf16[256,256]{1,0:T(8,128)(2,1)} %bitcast.16, bf16[2,512,256]{2,1,0:T(8,128)(2,1)} %enc_hbm.1), custom_call_target="tpu_custom_call" | custom-call | tf_op jit(solution)/shard_map/encode/pallas_call | solution.py:367
  2.6 5.1 %collective-permute-start.2 = (bf16[1,2,64,256]{3,2,1,0:T(8,128)(2,1)S(1)}, bf16[1,2,64,256]{3,2,1,0:T(8,128)(2,1)S(1)}, u32[]{:S(2)}, u32[]{:S(2)}) collective-permute-start(bf16[1,2,64,256]{3,2,1,0:T(8,128)(2,1)S(1)} %bitcast.12), channel_id=1, source_target_pairs={{0,24},{2,26},{4,28},{6,30},{8,16},{10,18},{12,20},{14,22},{16,8},... | collective-permute-start | bytes 196616 | tf_op jit(solution)/shard_map/ppermute | solution.py:331
  7.8 0.6 %collective-permute-start = (bf16[1,2,64,256]{3,2,1,0:T(8,128)(2,1)S(1)}, bf16[1,2,64,256]{3,2,1,0:T(8,128)(2,1)S(1)}, u32[]{:S(2)}, u32[]{:S(2)}) collective-permute-start(bf16[1,2,64,256]{3,2,1,0:T(8,128)(2,1)S(1)} %bitcast.14), channel_id=1, source_target_pairs={{0,8},{2,10},{4,12},{6,14},{8,0},{10,2},{12,4},{14,6},{16,24},{18,... | collective-permute-start | bytes 196616 | tf_op jit(solution)/shard_map/ppermute | solution.py:331
  8.4 1.8 %collective-permute-done.2.refs_3_ = bf16[1,2,64,256]{3,2,1,0:T(8,128)(2,1)S(1)} collective-permute-done((bf16[1,2,64,256]{3,2,1,0:T(8,128)(2,1)S(1)}, bf16[1,2,64,256]{3,2,1,0:T(8,128)(2,1)S(1)}, u32[]{:S(2)}, u32[]{:S(2)}) %collective-permute-start.2) | collective-permute-done | bytes 65568 | tf_op jit(solution)/shard_map/ppermute | solution.py:331
  10.3 3.1 %collective-permute-done.1.refs_2_ = bf16[1,2,64,256]{3,2,1,0:T(8,128)(2,1)S(1)} collective-permute-done((bf16[1,2,64,256]{3,2,1,0:T(8,128)(2,1)S(1)}, bf16[1,2,64,256]{3,2,1,0:T(8,128)(2,1)S(1)}, u32[]{:S(2)}, u32[]{:S(2)}) %collective-permute-start.1) | collective-permute-done | bytes 65568 | tf_op jit(solution)/shard_map/ppermute | solution.py:331
  13.4 2.5 %collective-permute-start.5 = (bf16[4,2,64,256]{3,2,1,0:T(8,128)(2,1)S(1)}, bf16[4,2,64,256]{3,2,1,0:T(8,128)(2,1)S(1)}, u32[]{:S(2)}, u32[]{:S(2)}) collective-permute-start(bf16[4,2,64,256]{3,2,1,0:T(8,128)(2,1)S(1)} %bitcast.8), channel_id=1, source_target_pairs={{0,6},{2,4},{4,2},{6,0},{8,14},{10,12},{12,10},{14,8},{16,22},{18,... | collective-permute-start | bytes 786440 | tf_op jit(solution)/shard_map/ppermute | solution.py:331
  15.9 0.5 collective-permute-start.4
  16.4 0.5 collective-permute-start.3
  17.0 6.6 %collective-permute-done.5.refs_3_ = bf16[4,2,64,256]{3,2,1,0:T(8,128)(2,1)S(1)} collective-permute-done((bf16[4,2,64,256]{3,2,1,0:T(8,128)(2,1)S(1)}, bf16[4,2,64,256]{3,2,1,0:T(8,128)(2,1)S(1)}, u32[]{:S(2)}, u32[]{:S(2)}) %collective-permute-start.5) | collective-permute-done | bytes 262176 | tf_op jit(solution)/shard_map/ppermute | solution.py:331
  23.6 4.3 %collective-permute-done.4.refs_2_ = bf16[4,2,64,256]{3,2,1,0:T(8,128)(2,1)S(1)} collective-permute-done((bf16[4,2,64,256]{3,2,1,0:T(8,128)(2,1)S(1)}, bf16[4,2,64,256]{3,2,1,0:T(8,128)(2,1)S(1)}, u32[]{:S(2)}, u32[]{:S(2)}) %collective-permute-start.4) | collective-permute-done | bytes 262176 | tf_op jit(solution)/shard_map/ppermute | solution.py:331
  27.9 0.2 collective-permute-done.3.refs_1_
  28.2 0.1 collective-permute-start.6
  28.2 4.0 %all-to-all-start = ((bf16[16,8,1024]{2,1,0:T(8,128)(2,1)}), bf16[16,8,1024]{2,1,0:T(8,128)(2,1)S(1)}, u32[]{:S(2)}, u32[]{:S(2)}) async-start(bf16[16,8,1024]{2,1,0:T(8,128)(2,1)} %get-tuple-element.15), calls=%async_computation | async-start | bytes 524288 | tf_op jit(solution)/shard_map/all_to_all | solution.py:384
  32.2 3.5 %tables.1 = (bf16[2,256,256]{2,1,0:T(8,128)(2,1)S(1)}, bf16[2,2,128,256]{3,2,1,0:T(8,128)(2,1)S(1)}, f32[4,256,128]{2,1,0:T(8,128)S(1)}, s32[232]{0:T(256)S(1)}) custom-call(s32[4,14]{1,0:T(4,128)} %list_ref.1, s32[4,14]{1,0:T(4,128)} %mask_ref.1, s32[1,64]{1,0:T(1,128)} %bitcast.17, f32[32,2,4,128]{3,2,1,0:T(4,128)} %kern_hbm.1, ...), custom_call_target="tpu_custom_call" | custom-call | tf_op jit(solution)/shard_map/tables/pallas_call | solution.py:394
  35.7 7.0 %all-to-all-done.coded_ref = bf16[16,8,1024]{2,1,0:T(8,128)(2,1)S(1)} async-done(((bf16[16,8,1024]{2,1,0:T(8,128)(2,1)}), bf16[16,8,1024]{2,1,0:T(8,128)(2,1)S(1)}, u32[]{:S(2)}, u32[]{:S(2)}) %all-to-all-start) | async-done | bytes 262176 | tf_op jit(solution)/shard_map/all_to_all | solution.py:384
  42.7 2.4 %far.1 = bf16[16,8,1024]{2,1,0:T(8,128)(2,1)} custom-call(bf16[16,8,1024]{2,1,0:T(8,128)(2,1)S(1)} %all-to-all-done.coded_ref, bf16[2,256,256]{2,1,0:T(8,128)(2,1)S(1)} %get-tuple-element.16.fwd_ref, bf16[2,2,128,256]{3,2,1,0:T(8,128)(2,1)S(1)} %get-tuple-element.17.inv_ref, f32[4,256,128]{2,1,0:T(8,128)S(1)} %get-tuple-element.18.spec_ref), custom_call_target="tpu_custom_call" | custom-call | tf_op jit(solution)/shard_map/far/pallas_call | solution.py:415
  45.1 3.5 %all-to-all-start.1 = ((bf16[16,8,1024]{2,1,0:T(8,128)(2,1)}), bf16[16,8,1024]{2,1,0:T(8,128)(2,1)S(1)}, u32[]{:S(2)}, u32[]{:S(2)}) async-start(bf16[16,8,1024]{2,1,0:T(8,128)(2,1)} %far.1), calls=%async_computation.1 | async-start | bytes 524288 | tf_op jit(solution)/shard_map/all_to_all | solution.py:423
  48.7 4.2 %near_mine.1 = (bf16[57,2,256,256]{3,2,1,0:T(8,128)(2,1)S(1)}, f32[256,256]{1,0:T(8,128)S(1)}) custom-call(s32[232]{0:T(256)S(1)} %get-tuple-element.19.order_ref, bf16[16,2,64,256]{3,2,1,0:T(8,128)(2,1)S(1)} %bitcast.7, bf16[4,14,2,256,256]{4,3,2,1,0:T(8,128)(2,1)} %blocks_hbm.1), custom_call_target="tpu_custom_call" | custom-call | tf_op jit(solution)/shard_map/near_mine/pallas_call | solution.py:427
  52.9 2.6 %near_theirs.1.near_ref = f32[256,256]{1,0:T(8,128)S(1)} custom-call(s32[232]{0:T(256)S(1)} %get-tuple-element.19.order_ref, bf16[16,2,64,256]{3,2,1,0:T(8,128)(2,1)S(1)} %collective-permute-done.6.src_ref, bf16[57,2,256,256]{3,2,1,0:T(8,128)(2,1)S(1)} %get-tuple-element.21.blk_ref, f32[256,256]{1,0:T(8,128)S(1)} %get-tuple-element.22.base_ref), custom_call_target="tpu_custom_call" | custom-call | tf_op jit(solution)/shard_map/near_theirs/pallas_call | solution.py:439
  55.5 2.7 %all-to-all-done.1.far_ref = bf16[16,8,1024]{2,1,0:T(8,128)(2,1)S(1)} async-done(((bf16[16,8,1024]{2,1,0:T(8,128)(2,1)}), bf16[16,8,1024]{2,1,0:T(8,128)(2,1)S(1)}, u32[]{:S(2)}, u32[]{:S(2)}) %all-to-all-start.1) | async-done | bytes 262176 | tf_op jit(solution)/shard_map/all_to_all | solution.py:423
  58.2 0.7 %decode.1 = (f32[256,128]{1,0:T(8,128)S(1)}, f32[256,128]{1,0:T(8,128)S(1)}) custom-call(bf16[16,8,1024]{2,1,0:T(8,128)(2,1)S(1)} %all-to-all-done.1.far_ref, bf16[2,512,256]{2,1,0:T(8,128)(2,1)S(1)} %copy-done, f32[256,256]{1,0:T(8,128)S(1)} %near_theirs.1.near_ref), custom_call_target="tpu_custom_call" | custom-call | tf_op jit(solution)/shard_map/decode/pallas_call | solution.py:450
  58.9 0.1 collective-permute-start.7
  58.9 1.3 %collective-permute-done.7 = f32[256,128]{1,0:T(8,128)S(1)} collective-permute-done((f32[256,128]{1,0:T(8,128)S(1)}, f32[256,128]{1,0:T(8,128)S(1)}, u32[]{:S(2)}, u32[]{:S(2)}) %collective-permute-start.7) | collective-permute-done | bytes 131104 | tf_op jit(solution)/shard_map/ppermute | solution.py:462
  60.3 0.7 %add.3 = f32[256,128]{1,0:T(8,128)} add(f32[256,128]{1,0:T(8,128)S(1)} %get-tuple-element.23, f32[256,128]{1,0:T(8,128)S(1)} %collective-permute-done.7) | non-fusion elementwise | flops 32768 | bytes 393216 | tf_op jit(solution)/shard_map/add | solution.py:463
  (7 shorter events, 0.1 us)
Async XLA Ops:
  2.6 7.6 %collective-permute-start.2 = (bf16[1,2,64,256]{3,2,1,0:T(8,128)(2,1)S(1)}, bf16[1,2,64,256]{3,2,1,0:T(8,128)(2,1)S(1)}, u32[]{:S(2)}, u32[]{:S(2)}) collective-permute-start(bf16[1,2,64,256]{3,2,1,0:T(8,128)(2,1)S(1)} %bitcast.12), channel_id=1, source_target_pairs={{0,24},{2,26},{4,28},{6,30},{8,16},{10,18},{12,20},{14,22},{16,8},... | collective-permute-start | bytes 196616 | tf_op jit(solution)/shard_map/ppermute | solution.py:331
  7.8 5.6 %collective-permute-start.1 = (bf16[1,2,64,256]{3,2,1,0:T(8,128)(2,1)S(1)}, bf16[1,2,64,256]{3,2,1,0:T(8,128)(2,1)S(1)}, u32[]{:S(2)}, u32[]{:S(2)}) collective-permute-start(bf16[1,2,64,256]{3,2,1,0:T(8,128)(2,1)S(1)} %bitcast.13), channel_id=1, source_target_pairs={{0,16},{2,18},{4,20},{6,22},{8,24},{10,26},{12,28},{14,30},{16,0},... | collective-permute-start | bytes 196616 | tf_op jit(solution)/shard_map/ppermute | solution.py:331
  7.8 5.6 %collective-permute-start = (bf16[1,2,64,256]{3,2,1,0:T(8,128)(2,1)S(1)}, bf16[1,2,64,256]{3,2,1,0:T(8,128)(2,1)S(1)}, u32[]{:S(2)}, u32[]{:S(2)}) collective-permute-start(bf16[1,2,64,256]{3,2,1,0:T(8,128)(2,1)S(1)} %bitcast.14), channel_id=1, source_target_pairs={{0,8},{2,10},{4,12},{6,14},{8,0},{10,2},{12,4},{14,6},{16,24},{18,... | collective-permute-start | bytes 196616 | tf_op jit(solution)/shard_map/ppermute | solution.py:331
  13.4 10.2 %collective-permute-start.5 = (bf16[4,2,64,256]{3,2,1,0:T(8,128)(2,1)S(1)}, bf16[4,2,64,256]{3,2,1,0:T(8,128)(2,1)S(1)}, u32[]{:S(2)}, u32[]{:S(2)}) collective-permute-start(bf16[4,2,64,256]{3,2,1,0:T(8,128)(2,1)S(1)} %bitcast.8), channel_id=1, source_target_pairs={{0,6},{2,4},{4,2},{6,0},{8,14},{10,12},{12,10},{14,8},{16,22},{18,... | collective-permute-start | bytes 786440 | tf_op jit(solution)/shard_map/ppermute | solution.py:331
  15.9 11.9 %collective-permute-start.4 = (bf16[4,2,64,256]{3,2,1,0:T(8,128)(2,1)S(1)}, bf16[4,2,64,256]{3,2,1,0:T(8,128)(2,1)S(1)}, u32[]{:S(2)}, u32[]{:S(2)}) collective-permute-start(bf16[4,2,64,256]{3,2,1,0:T(8,128)(2,1)S(1)} %bitcast.9), channel_id=1, source_target_pairs={{0,4},{2,6},{4,0},{6,2},{8,12},{10,14},{12,8},{14,10},{16,20},{18,... | collective-permute-start | bytes 786440 | tf_op jit(solution)/shard_map/ppermute | solution.py:331
  16.4 11.7 %collective-permute-start.3 = (bf16[4,2,64,256]{3,2,1,0:T(8,128)(2,1)S(1)}, bf16[4,2,64,256]{3,2,1,0:T(8,128)(2,1)S(1)}, u32[]{:S(2)}, u32[]{:S(2)}) collective-permute-start(bf16[4,2,64,256]{3,2,1,0:T(8,128)(2,1)S(1)} %bitcast.10), channel_id=1, source_target_pairs={{0,2},{2,0},{4,6},{6,4},{8,10},{10,8},{12,14},{14,12},{16,18},{18,... | collective-permute-start | bytes 786440 | tf_op jit(solution)/shard_map/ppermute | solution.py:331
  28.2 24.7 %collective-permute-start.6 = (bf16[16,2,64,256]{3,2,1,0:T(8,128)(2,1)S(1)}, bf16[16,2,64,256]{3,2,1,0:T(8,128)(2,1)S(1)}, u32[]{:S(2)}, u32[]{:S(2)}) collective-permute-start(bf16[16,2,64,256]{3,2,1,0:T(8,128)(2,1)S(1)} %bitcast.6), channel_id=1, source_target_pairs={{0,1},{1,0},{2,3},{3,2},{4,5},{5,4},{6,7},{7,6},{8,9},{9,8},{10,11... | collective-permute-start | bytes 3145736 | tf_op jit(solution)/shard_map/ppermute | solution.py:386
  28.2 14.5 %all-to-all-start = ((bf16[16,8,1024]{2,1,0:T(8,128)(2,1)}), bf16[16,8,1024]{2,1,0:T(8,128)(2,1)S(1)}, u32[]{:S(2)}, u32[]{:S(2)}) async-start(bf16[16,8,1024]{2,1,0:T(8,128)(2,1)} %get-tuple-element.15), calls=%async_computation | async-start | bytes 524288 | tf_op jit(solution)/shard_map/all_to_all | solution.py:384
  45.1 13.0 %all-to-all-start.1 = ((bf16[16,8,1024]{2,1,0:T(8,128)(2,1)}), bf16[16,8,1024]{2,1,0:T(8,128)(2,1)S(1)}, u32[]{:S(2)}, u32[]{:S(2)}) async-start(bf16[16,8,1024]{2,1,0:T(8,128)(2,1)} %far.1), calls=%async_computation.1 | async-start | bytes 524288 | tf_op jit(solution)/shard_map/all_to_all | solution.py:423
  48.7 9.5 %copy-start = (bf16[2,512,256]{2,1,0:T(8,128)(2,1)S(1)}, bf16[2,512,256]{2,1,0:T(8,128)(2,1)}, u32[]{:S(2)}) copy-start(bf16[2,512,256]{2,1,0:T(8,128)(2,1)} %dec_ref.1) | copy-start | bytes 1572868
  58.9 1.4 %collective-permute-start.7 = (f32[256,128]{1,0:T(8,128)S(1)}, f32[256,128]{1,0:T(8,128)S(1)}, u32[]{:S(2)}, u32[]{:S(2)}) collective-permute-start(f32[256,128]{1,0:T(8,128)S(1)} %get-tuple-element.24), channel_id=1, source_target_pairs={{0,1},{1,0},{2,3},{3,2},{4,5},{5,4},{6,7},{7,6},{8,9},{9,8},{10,11... | collective-permute-start | bytes 393224 | tf_op jit(solution)/shard_map/ppermute | solution.py:462

commit v3 on v2

--- a/solution.py
+++ b/solution.py
@@ -46,7 +46,7 @@
     return slice(start, start + rhs), slice(start + rhs, start + 2 * rhs)
 
 
-def encode_kernel(rhs, group, src_hbm, enc_hbm, out_ref, share_ref, src_ref, enc_ref, coded_ref, sem):
+def encode_kernel(rhs, group, src_hbm, enc_hbm, out_ref, whole_ref, share_ref, src_ref, enc_ref, coded_ref, sem):
     copies = [
         pltpu.make_async_copy(src_hbm, src_ref, sem.at[0]),
         pltpu.make_async_copy(enc_hbm.at[0], enc_ref.at[0], sem.at[1]),
@@ -56,6 +56,7 @@
         copy.start()
     copies[0].wait()
     src = src_ref[...]
+    whole_ref[...] = src
     part = src.shape[0] // lax.axis_size("dir")
     share_ref[...] = src_ref[pl.ds(pl.multiple_of(lax.axis_index("dir") * part, part), part), :]
     copies[1].wait()
@@ -174,18 +175,24 @@
     boxes, slots = list_ref.shape
     count = boxes * slots
     me, side = lax.axis_index("box"), lax.axis_index("dir")
+    rest = lax.axis_size("box") // 4
     for box in range(boxes):
 
         def visit(slot, filled):
             valid = mask_ref[box, slot] != 0
             source = list_ref[box, slot]
             owner, place = lax.div(source, boxes), lax.rem(source, boxes)
-            other = lax.div(place, share) != side
+            apart = owner ^ me
+            group, inner = lax.div(apart, rest), lax.rem(apart, rest)
+            in_half, whole_share = lax.rem(place, share), (group == 1) | (group == 2)
+            core = jnp.where(whole_share, group - 1, lax.div(place, share))
+            entry = jnp.where(whole_share, share + place, in_half + jnp.where(group == 3, share + boxes, 0))
+            other = core != side
             rank = box * slots + jnp.where(other, filled[1] + count, filled[0])
 
             @pl.when(valid)
             def _():
-                order_ref[rank] = (owner ^ me) * share + lax.rem(place, share)
+                order_ref[rank] = entry * rest + inner
                 order_ref[2 * count + rank] = box * slots + slot
 
             return (
@@ -211,7 +218,7 @@
         entries = [half * count + box * slots + rank for rank in ranks]
         places = [order_ref[2 * count + n] for n in entries]
         sources = [order_ref[n] for n in entries]
-        vectors = jnp.concatenate([src_ref[lax.div(n, src_ref.shape[1]), lax.rem(n, src_ref.shape[1])] for n in sources], axis=1)
+        vectors = jnp.concatenate([src_ref[n] for n in sources], axis=1)
         return [
             dot_nt(vectors, jnp.concatenate([blk_ref[place, part] for place in places], axis=1)) for part in range(2)
         ]
@@ -301,35 +308,45 @@
     other_ref[...] = jnp.where(first, right, left)
 
 
-def join_kernel(*refs):
+def stack_kernel(*refs):
     for n, ref in enumerate(refs[:-1]):
         refs[-1][:, n] = ref[...]
 
 
-def join(pieces):
-    shape = pieces[0].shape
-    joined = pl.pallas_call(
-        join_kernel,
-        out_shape=pltpu.VMEM((shape[0], len(pieces)) + shape[1:], pieces[0].dtype),
+def lay_kernel(*refs):
+    start = 0
+    for ref in refs[:-1]:
+        refs[-1][start : start + ref.shape[0]] = ref[...]
+        start += ref.shape[0]
+
+
+def join(kernel, pieces, shape):
+    return pl.pallas_call(
+        kernel,
+        out_shape=pltpu.VMEM(shape, pieces[0].dtype),
         in_specs=[vmem()] * len(pieces),
         out_specs=vmem(),
         compiler_params=budget(4),
         name="join",
     )(*pieces)
-    return joined.reshape((-1,) + shape[1:])
-
-
-def gather_shares(share):
+
+
+def gather_shares(boxes, share):
     size = lax.axis_size("box")
-    held = share[None]
-    low = size
-    while low > 1:
-        fan = 4 if low % 4 == 0 else 2
-        low //= fan
+    rest = size // 4
+    pairs = [(2 * i + core, 2 * (i ^ ((core + 1) * rest)) + core) for i in range(size) for core in range(2)]
+    whole = lax.ppermute(boxes, ("box", "dir"), pairs)
+    third = lax.ppermute(share, "box", [(i, i ^ (3 * rest)) for i in range(size)])
+    count = 2 * share.shape[0] + boxes.shape[0]
+    held = join(lay_kernel, [share, whole, third], (count,) + share.shape[1:])
+    while rest > 1:
+        fan = 4 if rest % 4 == 0 else 2
+        rest //= fan
         moved = [held]
         for delta in range(1, fan):
-            moved.append(lax.ppermute(held, "box", [(i, i ^ (delta * low)) for i in range(size)]))
-        held = join(moved)
+            moved.append(lax.ppermute(held, "box", [(i, i ^ (delta * rest)) for i in range(size)]))
+        count *= fan
+        held = join(stack_kernel, moved, (held.shape[0], fan) + share.shape[1:]).reshape((count,) + share.shape[1:])
     return held
 
 
@@ -364,14 +381,15 @@
     boxes = box_cell.shape[0]
 
     share = per_box // sides
-    coded, own_share = pl.pallas_call(
+    coded, own_boxes, own_share = pl.pallas_call(
         functools.partial(encode_kernel, rhs, group_dirs),
         out_shape=(
             pltpu.VMEM((owners, rows, width), BF16),
+            pltpu.VMEM((per_box * parts * rhs, unknowns), BF16),
             pltpu.VMEM((share * parts * rhs, unknowns), BF16),
         ),
         in_specs=[hbm(), hbm()],
-        out_specs=(vmem(),) * 2,
+        out_specs=(vmem(),) * 3,
         scratch_shapes=[
             pltpu.VMEM((rows * rhs, unknowns), BF16),
             pltpu.VMEM(encode.shape, BF16),
@@ -382,7 +400,7 @@
         name="encode",
     )(stay(sources.reshape(rows * rhs, unknowns)), stay(encode))
     arrived = lax.all_to_all(coded, "box", split_axis=0, concat_axis=0, tiled=True)
-    mine = gather_shares(own_share.reshape(share, parts * rhs, unknowns))
+    mine = gather_shares(own_boxes.reshape(per_box, parts * rhs, unknowns), own_share.reshape(share, parts * rhs, unknowns))
     theirs = lax.ppermute(mine, "dir", [(i, 1 - i) for i in range(sides)])
 
     cell = np.arange(GY * GZ)

time: 61.3 us -> 62.3 us (1.016)
  starting transfers between devices: 17 us -> 18.7 us
  waiting for transfers between devices: 27.1 us -> 26 us
    all_to_all x1, starting transfers between devices: 3.97 us -> 5.83 us  [whole_product(): lax.all_to_all(coded, 'box', split_axis=0, concat_axis=0, tiled=True)]
    ppermute x6 -> x5, waiting for transfers between devices: 16.1 us -> 15.3 us  [the longest x3 10.7 us: gather_shares(): lax.ppermute(held, 'box', [(i, i ^ delta * rest) for i in range(size)])]
    ppermute x6 -> x5, starting transfers between devices: 9.34 us -> 9.15 us  [the longest x3 3.55 us: gather_shares(): lax.ppermute(held, 'box', [(i, i ^ delta * rest) for i in range(size)])]
  transfers between devices with their start and end apart: 10 -> 9, of which waited for: 8 -> 7; matrix products, arithmetic and copies ran while one was open for 0% -> 0% of each run, Pallas kernels for 21% -> 21%
where the time goes in v3:
time: 62.3 us; the launch traced here: 61.9 us
  waiting for transfers between devices  26 us (42%)
  starting transfers between devices  18.7 us (30%)
  Pallas kernels  16.4 us (26%)
  other arithmetic  0.67 us (1%)
    ppermute x3, waiting for transfers between devices, gather_shares(): lax.ppermute(held, 'box', [(i, i ^ delta * rest) for i in range(size)])  10.7 us
    all_to_all x1, waiting for transfers between devices, whole_product(): lax.all_to_all(coded, 'box', split_axis=0, concat_axis=0, tiled=True)  6.66 us
    all_to_all x1, starting transfers between devices, whole_product(): lax.all_to_all(coded, 'box', split_axis=0, concat_axis=0, tiled=True)  5.83 us
    ppermute x1, waiting for transfers between devices, gather_shares(): third = lax.ppermute(share, 'box', [(i, i ^ 3 * rest) for i in range(size)])  4.65 us
    pallas_call x1, Pallas kernels, whole_product(): pl.pallas_call(functools.partial(near_mine_kernel, per_box), out_shape=(p...  4.17 us
    pallas_call x1, Pallas kernels, whole_product(): pl.pallas_call(functools.partial(table_kernel, grid_x, parts, share), out...  3.85 us
    ppermute x3, starting transfers between devices, gather_shares(): lax.ppermute(held, 'box', [(i, i ^ delta * rest) for i in range(size)])  3.55 us
    all_to_all x1, starting transfers between devices, whole_product(): lax.all_to_all(far, 'box', split_axis=0, concat_axis=0, tiled=True)  3.55 us
  transfers between devices with their start and end apart: 9, of which 7 were waited for; matrix products, arithmetic and copies ran while one was open for 0% of the time, Pallas kernels for 21%

profile of v3, /device:TPU:0, one launch (start us, length us, event | category | flops | bytes accessed | tf_op | source)
XLA Modules:
  0.0 61.9 jit_solution(2149281382899804035)
XLA Ops:
  0.0 2.6 %encode.1 = (bf16[16,8,1024]{2,1,0:T(8,128)(2,1)}, bf16[256,256]{1,0:T(8,128)(2,1)S(1)}, bf16[128,256]{1,0:T(8,128)(2,1)S(1)}) custom-call(bf16[256,256]{1,0:T(8,128)(2,1)} %bitcast.11, bf16[2,512,256]{2,1,0:T(8,128)(2,1)} %enc_hbm.1), custom_call_target="tpu_custom_call" | custom-call | tf_op jit(solution)/shard_map/encode/pallas_call | solution.py:384
  2.6 3.1 %collective-permute-start = (bf16[4,64,256]{2,1,0:T(8,128)(2,1)S(1)}, bf16[4,64,256]{2,1,0:T(8,128)(2,1)S(1)}, u32[]{:S(2)}, u32[]{:S(2)}) collective-permute-start(bf16[4,64,256]{2,1,0:T(8,128)(2,1)S(1)} %bitcast.10), channel_id=1, source_target_pairs={{0,8},{1,17},{2,10},{3,19},{4,12},{5,21},{6,14},{7,23},{8,0},{9,25... | collective-permute-start | bytes 393224 | tf_op jit(solution)/shard_map/ppermute | solution.py:338
  5.8 2.5 %collective-permute-start.1 = (bf16[2,64,256]{2,1,0:T(8,128)(2,1)S(1)}, bf16[2,64,256]{2,1,0:T(8,128)(2,1)S(1)}, u32[]{:S(2)}, u32[]{:S(2)}) collective-permute-start(bf16[2,64,256]{2,1,0:T(8,128)(2,1)S(1)} %bitcast.8), channel_id=1, source_target_pairs={{0,24},{2,26},{4,28},{6,30},{8,16},{10,18},{12,20},{14,22},{16,8},... | collective-permute-start | bytes 196616 | tf_op jit(solution)/shard_map/ppermute | solution.py:339
  8.2 4.6 %collective-permute-done.1.refs_2_ = bf16[2,64,256]{2,1,0:T(8,128)(2,1)S(1)} collective-permute-done((bf16[2,64,256]{2,1,0:T(8,128)(2,1)S(1)}, bf16[2,64,256]{2,1,0:T(8,128)(2,1)S(1)}, u32[]{:S(2)}, u32[]{:S(2)}) %collective-permute-start.1) | collective-permute-done | bytes 65568 | tf_op jit(solution)/shard_map/ppermute | solution.py:339
  12.9 2.5 %collective-permute-start.4 = (bf16[8,64,256]{2,1,0:T(8,128)(2,1)S(1)}, bf16[8,64,256]{2,1,0:T(8,128)(2,1)S(1)}, u32[]{:S(2)}, u32[]{:S(2)}) collective-permute-start(bf16[8,64,256]{2,1,0:T(8,128)(2,1)S(1)} %join.2.refs_0_), channel_id=1, source_target_pairs={{0,6},{2,4},{4,2},{6,0},{8,14},{10,12},{12,10},{14,8},{16,22},{18,... | collective-permute-start | bytes 786440 | tf_op jit(solution)/shard_map/ppermute | solution.py:347
  15.4 0.5 collective-permute-start.3
  15.9 0.5 collective-permute-start.2
  16.5 6.6 %collective-permute-done.4.refs_3_ = bf16[8,64,256]{2,1,0:T(8,128)(2,1)S(1)} collective-permute-done((bf16[8,64,256]{2,1,0:T(8,128)(2,1)S(1)}, bf16[8,64,256]{2,1,0:T(8,128)(2,1)S(1)}, u32[]{:S(2)}, u32[]{:S(2)}) %collective-permute-start.4) | collective-permute-done | bytes 262176 | tf_op jit(solution)/shard_map/ppermute | solution.py:347
  23.1 4.0 %collective-permute-done.3.refs_2_ = bf16[8,64,256]{2,1,0:T(8,128)(2,1)S(1)} collective-permute-done((bf16[8,64,256]{2,1,0:T(8,128)(2,1)S(1)}, bf16[8,64,256]{2,1,0:T(8,128)(2,1)S(1)}, u32[]{:S(2)}, u32[]{:S(2)}) %collective-permute-start.3) | collective-permute-done | bytes 262176 | tf_op jit(solution)/shard_map/ppermute | solution.py:347
  27.1 0.1 collective-permute-done.2.refs_1_
  27.1 0.1 join.3
  27.2 0.1 collective-permute-start.5
  27.3 5.8 %all-to-all-start = ((bf16[16,8,1024]{2,1,0:T(8,128)(2,1)}), bf16[16,8,1024]{2,1,0:T(8,128)(2,1)S(1)}, u32[]{:S(2)}, u32[]{:S(2)}) async-start(bf16[16,8,1024]{2,1,0:T(8,128)(2,1)} %get-tuple-element.16), calls=%async_computation | async-start | bytes 524288 | tf_op jit(solution)/shard_map/all_to_all | solution.py:402
  33.1 3.9 %tables.1 = (bf16[2,256,256]{2,1,0:T(8,128)(2,1)S(1)}, bf16[2,2,128,256]{3,2,1,0:T(8,128)(2,1)S(1)}, f32[4,256,128]{2,1,0:T(8,128)S(1)}, s32[232]{0:T(256)S(1)}) custom-call(s32[4,14]{1,0:T(4,128)} %list_ref.1, s32[4,14]{1,0:T(4,128)} %mask_ref.1, s32[1,64]{1,0:T(1,128)} %bitcast.12, f32[32,2,4,128]{3,2,1,0:T(4,128)} %kern_hbm.1, ...), custom_call_target="tpu_custom_call" | custom-call | tf_op jit(solution)/shard_map/tables/pallas_call | solution.py:412
  37.0 6.7 %all-to-all-done.coded_ref = bf16[16,8,1024]{2,1,0:T(8,128)(2,1)S(1)} async-done(((bf16[16,8,1024]{2,1,0:T(8,128)(2,1)}), bf16[16,8,1024]{2,1,0:T(8,128)(2,1)S(1)}, u32[]{:S(2)}, u32[]{:S(2)}) %all-to-all-start) | async-done | bytes 262176 | tf_op jit(solution)/shard_map/all_to_all | solution.py:402
  43.7 2.4 %far.1 = bf16[16,8,1024]{2,1,0:T(8,128)(2,1)} custom-call(bf16[16,8,1024]{2,1,0:T(8,128)(2,1)S(1)} %all-to-all-done.coded_ref, bf16[2,256,256]{2,1,0:T(8,128)(2,1)S(1)} %get-tuple-element.17.fwd_ref, bf16[2,2,128,256]{3,2,1,0:T(8,128)(2,1)S(1)} %get-tuple-element.18.inv_ref, f32[4,256,128]{2,1,0:T(8,128)S(1)} %get-tuple-element.19.spec_ref), custom_call_target="tpu_custom_call" | custom-call | tf_op jit(solution)/shard_map/far/pallas_call | solution.py:433
  46.0 3.6 %all-to-all-start.1 = ((bf16[16,8,1024]{2,1,0:T(8,128)(2,1)}), bf16[16,8,1024]{2,1,0:T(8,128)(2,1)S(1)}, u32[]{:S(2)}, u32[]{:S(2)}) async-start(bf16[16,8,1024]{2,1,0:T(8,128)(2,1)} %far.1), calls=%async_computation.1 | async-start | bytes 524288 | tf_op jit(solution)/shard_map/all_to_all | solution.py:441
  49.6 4.2 %near_mine.1 = (bf16[57,2,256,256]{3,2,1,0:T(8,128)(2,1)S(1)}, f32[256,256]{1,0:T(8,128)S(1)}) custom-call(s32[232]{0:T(256)S(1)} %get-tuple-element.20.order_ref, bf16[32,64,256]{2,1,0:T(8,128)(2,1)S(1)} %bitcast.7, bf16[4,14,2,256,256]{4,3,2,1,0:T(8,128)(2,1)} %blocks_hbm.1), custom_call_target="tpu_custom_call" | custom-call | tf_op jit(solution)/shard_map/near_mine/pallas_call | solution.py:445
  53.8 2.6 %near_theirs.1.near_ref = f32[256,256]{1,0:T(8,128)S(1)} custom-call(s32[232]{0:T(256)S(1)} %get-tuple-element.20.order_ref, bf16[32,64,256]{2,1,0:T(8,128)(2,1)S(1)} %collective-permute-done.5.src_ref, bf16[57,2,256,256]{3,2,1,0:T(8,128)(2,1)S(1)} %get-tuple-element.23.blk_ref, f32[256,256]{1,0:T(8,128)S(1)} %get-tuple-element.24.base_ref), custom_call_target="tpu_custom_call" | custom-call | tf_op jit(solution)/shard_map/near_theirs/pallas_call | solution.py:457
  56.4 2.7 %all-to-all-done.1.far_ref = bf16[16,8,1024]{2,1,0:T(8,128)(2,1)S(1)} async-done(((bf16[16,8,1024]{2,1,0:T(8,128)(2,1)}), bf16[16,8,1024]{2,1,0:T(8,128)(2,1)S(1)}, u32[]{:S(2)}, u32[]{:S(2)}) %all-to-all-start.1) | async-done | bytes 262176 | tf_op jit(solution)/shard_map/all_to_all | solution.py:441
  59.1 0.7 %decode.1 = (f32[256,128]{1,0:T(8,128)S(1)}, f32[256,128]{1,0:T(8,128)S(1)}) custom-call(bf16[16,8,1024]{2,1,0:T(8,128)(2,1)S(1)} %all-to-all-done.1.far_ref, bf16[2,512,256]{2,1,0:T(8,128)(2,1)S(1)} %copy-done, f32[256,256]{1,0:T(8,128)S(1)} %near_theirs.1.near_ref), custom_call_target="tpu_custom_call" | custom-call | tf_op jit(solution)/shard_map/decode/pallas_call | solution.py:468
  59.8 0.1 collective-permute-start.6
  59.9 1.3 %collective-permute-done.6 = f32[256,128]{1,0:T(8,128)S(1)} collective-permute-done((f32[256,128]{1,0:T(8,128)S(1)}, f32[256,128]{1,0:T(8,128)S(1)}, u32[]{:S(2)}, u32[]{:S(2)}) %collective-permute-start.6) | collective-permute-done | bytes 131104 | tf_op jit(solution)/shard_map/ppermute | solution.py:480
  61.2 0.7 %add.3 = f32[256,128]{1,0:T(8,128)} add(f32[256,128]{1,0:T(8,128)S(1)} %get-tuple-element.25, f32[256,128]{1,0:T(8,128)S(1)} %collective-permute-done.6) | non-fusion elementwise | flops 32768 | bytes 393216 | tf_op jit(solution)/shard_map/add | solution.py:481
  (5 shorter events, 0.0 us)
Async XLA Ops:
  2.6 10.2 %collective-permute-start = (bf16[4,64,256]{2,1,0:T(8,128)(2,1)S(1)}, bf16[4,64,256]{2,1,0:T(8,128)(2,1)S(1)}, u32[]{:S(2)}, u32[]{:S(2)}) collective-permute-start(bf16[4,64,256]{2,1,0:T(8,128)(2,1)S(1)} %bitcast.10), channel_id=1, source_target_pairs={{0,8},{1,17},{2,10},{3,19},{4,12},{5,21},{6,14},{7,23},{8,0},{9,25... | collective-permute-start | bytes 393224 | tf_op jit(solution)/shard_map/ppermute | solution.py:338
  5.8 7.1 %collective-permute-start.1 = (bf16[2,64,256]{2,1,0:T(8,128)(2,1)S(1)}, bf16[2,64,256]{2,1,0:T(8,128)(2,1)S(1)}, u32[]{:S(2)}, u32[]{:S(2)}) collective-permute-start(bf16[2,64,256]{2,1,0:T(8,128)(2,1)S(1)} %bitcast.8), channel_id=1, source_target_pairs={{0,24},{2,26},{4,28},{6,30},{8,16},{10,18},{12,20},{14,22},{16,8},... | collective-permute-start | bytes 196616 | tf_op jit(solution)/shard_map/ppermute | solution.py:339
  12.9 10.2 %collective-permute-start.4 = (bf16[8,64,256]{2,1,0:T(8,128)(2,1)S(1)}, bf16[8,64,256]{2,1,0:T(8,128)(2,1)S(1)}, u32[]{:S(2)}, u32[]{:S(2)}) collective-permute-start(bf16[8,64,256]{2,1,0:T(8,128)(2,1)S(1)} %join.2.refs_0_), channel_id=1, source_target_pairs={{0,6},{2,4},{4,2},{6,0},{8,14},{10,12},{12,10},{14,8},{16,22},{18,... | collective-permute-start | bytes 786440 | tf_op jit(solution)/shard_map/ppermute | solution.py:347
  15.4 11.6 %collective-permute-start.3 = (bf16[8,64,256]{2,1,0:T(8,128)(2,1)S(1)}, bf16[8,64,256]{2,1,0:T(8,128)(2,1)S(1)}, u32[]{:S(2)}, u32[]{:S(2)}) collective-permute-start(bf16[8,64,256]{2,1,0:T(8,128)(2,1)S(1)} %join.2.refs_0_), channel_id=1, source_target_pairs={{0,4},{2,6},{4,0},{6,2},{8,12},{10,14},{12,8},{14,10},{16,20},{18,... | collective-permute-start | bytes 786440 | tf_op jit(solution)/shard_map/ppermute | solution.py:347
  15.9 11.2 %collective-permute-start.2 = (bf16[8,64,256]{2,1,0:T(8,128)(2,1)S(1)}, bf16[8,64,256]{2,1,0:T(8,128)(2,1)S(1)}, u32[]{:S(2)}, u32[]{:S(2)}) collective-permute-start(bf16[8,64,256]{2,1,0:T(8,128)(2,1)S(1)} %join.2.refs_0_), channel_id=1, source_target_pairs={{0,2},{2,0},{4,6},{6,4},{8,10},{10,8},{12,14},{14,12},{16,18},{18,... | collective-permute-start | bytes 786440 | tf_op jit(solution)/shard_map/ppermute | solution.py:347
  27.2 26.6 %collective-permute-start.5 = (bf16[32,64,256]{2,1,0:T(8,128)(2,1)S(1)}, bf16[32,64,256]{2,1,0:T(8,128)(2,1)S(1)}, u32[]{:S(2)}, u32[]{:S(2)}) collective-permute-start(bf16[32,64,256]{2,1,0:T(8,128)(2,1)S(1)} %bitcast.6), channel_id=1, source_target_pairs={{0,1},{1,0},{2,3},{3,2},{4,5},{5,4},{6,7},{7,6},{8,9},{9,8},{10,11... | collective-permute-start | bytes 3145736 | tf_op jit(solution)/shard_map/ppermute | solution.py:404
  27.3 16.4 %all-to-all-start = ((bf16[16,8,1024]{2,1,0:T(8,128)(2,1)}), bf16[16,8,1024]{2,1,0:T(8,128)(2,1)S(1)}, u32[]{:S(2)}, u32[]{:S(2)}) async-start(bf16[16,8,1024]{2,1,0:T(8,128)(2,1)} %get-tuple-element.16), calls=%async_computation | async-start | bytes 524288 | tf_op jit(solution)/shard_map/all_to_all | solution.py:402
  46.0 13.0 %all-to-all-start.1 = ((bf16[16,8,1024]{2,1,0:T(8,128)(2,1)}), bf16[16,8,1024]{2,1,0:T(8,128)(2,1)S(1)}, u32[]{:S(2)}, u32[]{:S(2)}) async-start(bf16[16,8,1024]{2,1,0:T(8,128)(2,1)} %far.1), calls=%async_computation.1 | async-start | bytes 524288 | tf_op jit(solution)/shard_map/all_to_all | solution.py:441
  49.6 9.5 %copy-start = (bf16[2,512,256]{2,1,0:T(8,128)(2,1)S(1)}, bf16[2,512,256]{2,1,0:T(8,128)(2,1)}, u32[]{:S(2)}) copy-start(bf16[2,512,256]{2,1,0:T(8,128)(2,1)} %dec_ref.1) | copy-start | bytes 1572868
  59.8 1.4 %collective-permute-start.6 = (f32[256,128]{1,0:T(8,128)S(1)}, f32[256,128]{1,0:T(8,128)S(1)}, u32[]{:S(2)}, u32[]{:S(2)}) collective-permute-start(f32[256,128]{1,0:T(8,128)S(1)} %get-tuple-element.26), channel_id=1, source_target_pairs={{0,1},{1,0},{2,3},{3,2},{4,5},{5,4},{6,7},{7,6},{8,9},{9,8},{10,11... | collective-permute-start | bytes 393224 | tf_op jit(solution)/shard_map/ppermute | solution.py:480

commit v4 on v3

--- a/solution.py
+++ b/solution.py
@@ -13,6 +13,7 @@
 GY = 8
 GZ = 4
 LANES = 128
+PACK = 1 << 16
 
 F32 = jnp.float32
 BF16 = jnp.bfloat16
@@ -83,18 +84,22 @@
 
 
 def table_kernel(
-    grid_x, parts, share, list_ref, mask_ref, box_hbm, kern_hbm, cell_hbm, full_hbm,
-    fwd_ref, inv_ref, spec_ref, order_ref, box_ref, kern_ref, cell_ref, full_ref, sem,
+    grid_x, parts, share, list_hbm, mask_hbm, box_hbm, kern_hbm, cell_hbm, full_hbm,
+    fwd_ref, inv_ref, spec_ref, order_ref, list_ref, mask_ref, box_ref, kern_ref, cell_ref, full_ref, sem,
 ):
     copies = [
         pltpu.make_async_copy(box_hbm, box_ref, sem.at[0]),
         pltpu.make_async_copy(cell_hbm, cell_ref, sem.at[1]),
         pltpu.make_async_copy(kern_hbm, kern_ref, sem.at[2]),
         pltpu.make_async_copy(full_hbm, full_ref, sem.at[3]),
+        pltpu.make_async_copy(list_hbm, list_ref, sem.at[4]),
+        pltpu.make_async_copy(mask_hbm, mask_ref, sem.at[5]),
     ]
     for copy in copies:
         copy.start()
-    list_slots(share, list_ref, mask_ref, order_ref)
+    copies[4].wait()
+    copies[5].wait()
+    list_slots(share, list_ref[...], mask_ref[...], order_ref)
     full_hi, full_lo = full_ref.at[0], full_ref.at[1]
     cell_hi, cell_lo = cell_ref.at[0], cell_ref.at[1]
     plane = full_hi.shape[0] // 2
@@ -171,43 +176,29 @@
         out_ref[:, :, cols] = total.astype(BF16).reshape(owners, rows, step)
 
 
-def list_slots(share, list_ref, mask_ref, order_ref):
-    boxes, slots = list_ref.shape
-    count = boxes * slots
+def list_slots(share, near_list, near_mask, order_ref):
+    boxes, slots = near_list.shape
     me, side = lax.axis_index("box"), lax.axis_index("dir")
     rest = lax.axis_size("box") // 4
-    for box in range(boxes):
-
-        def visit(slot, filled):
-            valid = mask_ref[box, slot] != 0
-            source = list_ref[box, slot]
-            owner, place = lax.div(source, boxes), lax.rem(source, boxes)
-            apart = owner ^ me
-            group, inner = lax.div(apart, rest), lax.rem(apart, rest)
-            in_half, whole_share = lax.rem(place, share), (group == 1) | (group == 2)
-            core = jnp.where(whole_share, group - 1, lax.div(place, share))
-            entry = jnp.where(whole_share, share + place, in_half + jnp.where(group == 3, share + boxes, 0))
-            other = core != side
-            rank = box * slots + jnp.where(other, filled[1] + count, filled[0])
-
-            @pl.when(valid)
-            def _():
-                order_ref[rank] = entry * rest + inner
-                order_ref[2 * count + rank] = box * slots + slot
-
-            return (
-                filled[0] + (valid & ~other).astype(jnp.int32),
-                filled[1] + (valid & other).astype(jnp.int32),
-            )
-
-        filled = lax.fori_loop(0, slots, visit, (jnp.int32(0), jnp.int32(0)))
-        for half in range(2):
-            order_ref[4 * count + half * boxes + box] = filled[half]
-
-            @pl.loop(filled[half], slots)
-            def _(rank):
-                order_ref[half * count + box * slots + rank] = 0
-                order_ref[(2 + half) * count + box * slots + rank] = count
+    source = jnp.concatenate([near_list, near_list], axis=0)
+    valid = jnp.concatenate([near_mask, near_mask], axis=0) != 0
+    apart, place = (source // boxes) ^ me, source % boxes
+    group, inner = apart // rest, apart % rest
+    in_half, whole_share = place % share, group >= 2
+    core = jnp.where(whole_share, 3 - group, place // share)
+    entry = jnp.where(whole_share, share + place, in_half + jnp.where(group == 1, share + boxes, 0)) * rest + inner
+    row = lax.broadcasted_iota(jnp.int32, source.shape, 0)
+    used = jnp.where(valid & ((core == side) == (row < boxes)), 1, 0)
+    rank = lax.broadcasted_iota(jnp.int32, order_ref.shape, 1)
+    entry = entry + (row % boxes) * (slots * PACK)
+    order = jnp.full_like(rank, boxes * slots * PACK)
+    filled = jnp.zeros((2 * boxes, 1), jnp.int32)
+    for slot in range(slots):
+        here = used[:, slot : slot + 1]
+        hit = (rank == filled) & (here != 0)
+        order = jnp.where(hit, entry[:, slot : slot + 1] + slot * PACK, order)
+        filled = filled + here
+    order_ref[...] = jnp.where(rank == slots, filled, order)
 
 
 def near_products(half, boxes, order_ref, src_ref, blk_ref, acc, arrived):
@@ -215,25 +206,27 @@
     slots = count // boxes
 
     def product(box, ranks):
-        entries = [half * count + box * slots + rank for rank in ranks]
-        places = [order_ref[2 * count + n] for n in entries]
-        sources = [order_ref[n] for n in entries]
+        row = half * boxes + box
+        packed = [order_ref[row, rank] for rank in ranks]
+        places = [lax.div(entry, PACK) for entry in packed]
+        sources = [lax.rem(entry, PACK) for entry in packed]
         vectors = jnp.concatenate([src_ref[n] for n in sources], axis=1)
         return [
             dot_nt(vectors, jnp.concatenate([blk_ref[place, part] for place in places], axis=1)) for part in range(2)
         ]
 
-    first = min(6, slots)
+    first = min(5, slots)
     for box in range(boxes):
         arrived(box)
         acc[box, 0], acc[box, 1] = product(box, range(first))
-    for box in range(boxes):
-
-        @pl.when(order_ref[4 * count + half * boxes + box] > first)
-        def _():
-            more = product(box, range(first, slots))
-            acc[box, 0] += more[0]
-            acc[box, 1] += more[1]
+    for start in range(first, slots, 3):
+        for box in range(boxes):
+
+            @pl.when(order_ref[half * boxes + box, slots] > start)
+            def _():
+                more = product(box, range(start, min(start + 3, slots)))
+                acc[box, 0] += more[0]
+                acc[box, 1] += more[1]
 
 
 def near_mine_kernel(boxes, order_ref, src_ref, blocks_hbm, blk_ref, out_ref, acc, sem):
@@ -241,7 +234,7 @@
     slots = count // boxes
 
     def block_copy(half, box, rank):
-        place = order_ref[(2 + half) * count + box * slots + rank]
+        place = lax.div(order_ref[half * boxes + box, rank], PACK)
         return pltpu.make_async_copy(
             blocks_hbm.at[box, place - box * slots], blk_ref.at[place], sem.at[half * boxes + box]
         )
@@ -249,14 +242,14 @@
     for half in range(2):
         for box in range(boxes):
 
-            @pl.loop(0, order_ref[4 * count + half * boxes + box])
+            @pl.loop(0, order_ref[half * boxes + box, slots])
             def _(rank):
                 block_copy(half, box, rank).start()
 
     blk_ref[count] = jnp.zeros(blk_ref.shape[1:], BF16)
 
     def arrived(half, box):
-        @pl.loop(0, order_ref[4 * count + half * boxes + box])
+        @pl.loop(0, order_ref[half * boxes + box, slots])
         def _(rank):
             block_copy(half, box, rank).wait()
 
@@ -334,9 +327,9 @@
 def gather_shares(boxes, share):
     size = lax.axis_size("box")
     rest = size // 4
-    pairs = [(2 * i + core, 2 * (i ^ ((core + 1) * rest)) + core) for i in range(size) for core in range(2)]
+    pairs = [(2 * i + core, 2 * (i ^ ((3 - core) * rest)) + core) for i in range(size) for core in range(2)]
     whole = lax.ppermute(boxes, ("box", "dir"), pairs)
-    third = lax.ppermute(share, "box", [(i, i ^ (3 * rest)) for i in range(size)])
+    third = lax.ppermute(share, "box", [(i, i ^ rest) for i in range(size)])
     count = 2 * share.shape[0] + boxes.shape[0]
     held = join(lay_kernel, [share, whole, third], (count,) + share.shape[1:])
     while rest > 1:
@@ -415,16 +408,18 @@
             pltpu.VMEM((grid_x, 2 * plane, 2 * parts * boxes), BF16),
             pltpu.VMEM((grid_x, 2, parts * boxes, 2 * plane), BF16),
             pltpu.VMEM((double_x, 2 * plane, LANES), F32),
-            jax.ShapeDtypeStruct((4 * count + 2 * per_box,), jnp.int32),
+            jax.ShapeDtypeStruct((2 * per_box, LANES), jnp.int32),
         ),
-        in_specs=[smem(), smem()] + [hbm()] * 4,
-        out_specs=(vmem(), vmem(), vmem(), smem()),
+        in_specs=[hbm()] * 6,
+        out_specs=(vmem(),) * 4,
         scratch_shapes=[
+            pltpu.VMEM(near_list.shape, jnp.int32),
+            pltpu.VMEM(near_mask.shape, jnp.int32),
             pltpu.VMEM((1, boxes), jnp.int32),
             pltpu.VMEM(kernel.shape, F32),
             pltpu.VMEM(constants[0].shape, BF16),
             pltpu.VMEM(constants[1].shape, BF16),
-            pltpu.SemaphoreType.DMA((4,)),
+            pltpu.SemaphoreType.DMA((6,)),
         ],
         compiler_params=budget(24),
         name="tables",

time: 62.3 us -> 62 us (level)
  Pallas kernels: 16.4 us -> 14.3 us
  waiting for transfers between devices: 26 us -> 27.8 us
    ppermute x1, starting transfers between devices: 2.47 us -> 0.01 us  [gather_shares(): third = lax.ppermute(share, 'box', [(i, i ^ rest) for i in range(size)])]
    ppermute x1, starting transfers between devices: 3.12 us -> 5.14 us  [gather_shares(): whole = lax.ppermute(boxes, ('box', 'dir'), pairs)]
    pallas_call x1, Pallas kernels: 3.85 us -> 2.13 us  [whole_product(): pl.pallas_call(functools.partial(table_kernel, grid_x, parts, share), out...]
    all_to_all x1, waiting for transfers between devices: 6.66 us -> 8.07 us  [whole_product(): lax.all_to_all(coded, 'box', split_axis=0, concat_axis=0, tiled=True)]
  transfers between devices with their start and end apart: 9 -> 9, of which waited for: 7 -> 7; matrix products, arithmetic and copies ran while one was open for 0% -> 0% of each run, Pallas kernels for 21% -> 18%
where the time goes in v4:
time: 62 us; the launch traced here: 61.6 us
  waiting for transfers between devices  27.8 us (45%)
  starting transfers between devices  18.8 us (30%)
  Pallas kernels  14.3 us (23%)
  other arithmetic  0.67 us (1%)
    ppermute x3, waiting for transfers between devices, gather_shares(): lax.ppermute(held, 'box', [(i, i ^ delta * rest) for i in range(size)])  10.6 us
    all_to_all x1, waiting for transfers between devices, whole_product(): lax.all_to_all(coded, 'box', split_axis=0, concat_axis=0, tiled=True)  8.07 us
    all_to_all x1, starting transfers between devices, whole_product(): lax.all_to_all(coded, 'box', split_axis=0, concat_axis=0, tiled=True)  6.4 us
    ppermute x1, starting transfers between devices, gather_shares(): whole = lax.ppermute(boxes, ('box', 'dir'), pairs)  5.14 us
    ppermute x1, waiting for transfers between devices, gather_shares(): third = lax.ppermute(share, 'box', [(i, i ^ rest) for i in range(size)])  4.76 us
    pallas_call x1, Pallas kernels, whole_product(): pl.pallas_call(functools.partial(near_mine_kernel, per_box), out_shape=(p...  3.98 us
    ppermute x3, starting transfers between devices, gather_shares(): lax.ppermute(held, 'box', [(i, i ^ delta * rest) for i in range(size)])  3.55 us
    all_to_all x1, starting transfers between devices, whole_product(): lax.all_to_all(far, 'box', split_axis=0, concat_axis=0, tiled=True)  3.54 us
  transfers between devices with their start and end apart: 9, of which 7 were waited for; matrix products, arithmetic and copies ran while one was open for 0% of the time, Pallas kernels for 18%

profile of v4, /device:TPU:0, one launch (start us, length us, event | category | flops | bytes accessed | tf_op | source)
XLA Modules:
  0.0 61.6 jit_solution(17094323306330304749)
XLA Ops:
  0.0 2.6 %encode.1 = (bf16[16,8,1024]{2,1,0:T(8,128)(2,1)}, bf16[256,256]{1,0:T(8,128)(2,1)S(1)}, bf16[128,256]{1,0:T(8,128)(2,1)S(1)}) custom-call(bf16[256,256]{1,0:T(8,128)(2,1)} %bitcast.11, bf16[2,512,256]{2,1,0:T(8,128)(2,1)} %enc_hbm.1), custom_call_target="tpu_custom_call" | custom-call | tf_op jit(solution)/shard_map/encode/pallas_call | solution.py:377
  2.6 5.1 %collective-permute-start = (bf16[4,64,256]{2,1,0:T(8,128)(2,1)S(1)}, bf16[4,64,256]{2,1,0:T(8,128)(2,1)S(1)}, u32[]{:S(2)}, u32[]{:S(2)}) collective-permute-start(bf16[4,64,256]{2,1,0:T(8,128)(2,1)S(1)} %bitcast.10), channel_id=1, source_target_pairs={{0,24},{1,17},{2,26},{3,19},{4,28},{5,21},{6,30},{7,23},{8,16},{9,... | collective-permute-start | bytes 393224 | tf_op jit(solution)/shard_map/ppermute | solution.py:331
  7.8 4.8 %collective-permute-done.1.refs_2_ = bf16[2,64,256]{2,1,0:T(8,128)(2,1)S(1)} collective-permute-done((bf16[2,64,256]{2,1,0:T(8,128)(2,1)S(1)}, bf16[2,64,256]{2,1,0:T(8,128)(2,1)S(1)}, u32[]{:S(2)}, u32[]{:S(2)}) %collective-permute-start.1) | collective-permute-done | bytes 65568 | tf_op jit(solution)/shard_map/ppermute | solution.py:332
  12.6 2.6 %collective-permute-start.4 = (bf16[8,64,256]{2,1,0:T(8,128)(2,1)S(1)}, bf16[8,64,256]{2,1,0:T(8,128)(2,1)S(1)}, u32[]{:S(2)}, u32[]{:S(2)}) collective-permute-start(bf16[8,64,256]{2,1,0:T(8,128)(2,1)S(1)} %join.2.refs_0_), channel_id=1, source_target_pairs={{0,6},{2,4},{4,2},{6,0},{8,14},{10,12},{12,10},{14,8},{16,22},{18,... | collective-permute-start | bytes 786440 | tf_op jit(solution)/shard_map/ppermute | solution.py:340
  15.2 0.5 collective-permute-start.3
  15.7 0.4 collective-permute-start.2
  16.1 6.6 %collective-permute-done.4.refs_3_ = bf16[8,64,256]{2,1,0:T(8,128)(2,1)S(1)} collective-permute-done((bf16[8,64,256]{2,1,0:T(8,128)(2,1)S(1)}, bf16[8,64,256]{2,1,0:T(8,128)(2,1)S(1)}, u32[]{:S(2)}, u32[]{:S(2)}) %collective-permute-start.4) | collective-permute-done | bytes 262176 | tf_op jit(solution)/shard_map/ppermute | solution.py:340
  22.8 3.8 %collective-permute-done.3.refs_2_ = bf16[8,64,256]{2,1,0:T(8,128)(2,1)S(1)} collective-permute-done((bf16[8,64,256]{2,1,0:T(8,128)(2,1)S(1)}, bf16[8,64,256]{2,1,0:T(8,128)(2,1)S(1)}, u32[]{:S(2)}, u32[]{:S(2)}) %collective-permute-start.3) | collective-permute-done | bytes 262176 | tf_op jit(solution)/shard_map/ppermute | solution.py:340
  26.6 0.1 collective-permute-done.2.refs_1_
  26.7 0.1 join.3
  26.8 0.1 collective-permute-start.5
  26.8 6.4 %all-to-all-start = ((bf16[16,8,1024]{2,1,0:T(8,128)(2,1)}), bf16[16,8,1024]{2,1,0:T(8,128)(2,1)S(1)}, u32[]{:S(2)}, u32[]{:S(2)}) async-start(bf16[16,8,1024]{2,1,0:T(8,128)(2,1)} %get-tuple-element.16), calls=%async_computation | async-start | bytes 524288 | tf_op jit(solution)/shard_map/all_to_all | solution.py:395
  33.2 2.1 %tables.1 = (bf16[2,256,256]{2,1,0:T(8,128)(2,1)S(1)}, bf16[2,2,128,256]{3,2,1,0:T(8,128)(2,1)S(1)}, f32[4,256,128]{2,1,0:T(8,128)S(1)}, s32[8,128]{1,0:T(8,128)S(1)}) custom-call(s32[4,14]{1,0:T(4,128)} %list_hbm.1, s32[4,14]{1,0:T(4,128)} %mask_hbm.1, s32[1,64]{1,0:T(1,128)} %bitcast.12, f32[32,2,4,128]{3,2,1,0:T(4,128)} %kern_hbm.1, ...), custom_call_target="tpu_custom_call" | custom-call | tf_op jit(solution)/shard_map/tables/pallas_call | solution.py:405
  35.4 8.1 %all-to-all-done.coded_ref = bf16[16,8,1024]{2,1,0:T(8,128)(2,1)S(1)} async-done(((bf16[16,8,1024]{2,1,0:T(8,128)(2,1)}), bf16[16,8,1024]{2,1,0:T(8,128)(2,1)S(1)}, u32[]{:S(2)}, u32[]{:S(2)}) %all-to-all-start) | async-done | bytes 262176 | tf_op jit(solution)/shard_map/all_to_all | solution.py:395
  43.5 2.4 %far.1 = bf16[16,8,1024]{2,1,0:T(8,128)(2,1)} custom-call(bf16[16,8,1024]{2,1,0:T(8,128)(2,1)S(1)} %all-to-all-done.coded_ref, bf16[2,256,256]{2,1,0:T(8,128)(2,1)S(1)} %get-tuple-element.17.fwd_ref, bf16[2,2,128,256]{3,2,1,0:T(8,128)(2,1)S(1)} %get-tuple-element.18.inv_ref, f32[4,256,128]{2,1,0:T(8,128)S(1)} %get-tuple-element.19.spec_ref), custom_call_target="tpu_custom_call" | custom-call | tf_op jit(solution)/shard_map/far/pallas_call | solution.py:428
  45.8 3.5 %all-to-all-start.1 = ((bf16[16,8,1024]{2,1,0:T(8,128)(2,1)}), bf16[16,8,1024]{2,1,0:T(8,128)(2,1)S(1)}, u32[]{:S(2)}, u32[]{:S(2)}) async-start(bf16[16,8,1024]{2,1,0:T(8,128)(2,1)} %far.1), calls=%async_computation.1 | async-start | bytes 524288 | tf_op jit(solution)/shard_map/all_to_all | solution.py:436
  49.4 0.0 copy-start
  49.4 4.0 %near_mine.1 = (bf16[57,2,256,256]{3,2,1,0:T(8,128)(2,1)S(1)}, f32[256,256]{1,0:T(8,128)S(1)}) custom-call(s32[8,128]{1,0:T(8,128)S(1)} %get-tuple-element.20.order_ref, bf16[32,64,256]{2,1,0:T(8,128)(2,1)S(1)} %bitcast.7, bf16[4,14,2,256,256]{4,3,2,1,0:T(8,128)(2,1)} %blocks_hbm.1), custom_call_target="tpu_custom_call" | custom-call | tf_op jit(solution)/shard_map/near_mine/pallas_call | solution.py:440
  53.4 2.4 %near_theirs.1.near_ref = f32[256,256]{1,0:T(8,128)S(1)} custom-call(s32[8,128]{1,0:T(8,128)S(1)} %get-tuple-element.20.order_ref, bf16[32,64,256]{2,1,0:T(8,128)(2,1)S(1)} %collective-permute-done.5.src_ref, bf16[57,2,256,256]{3,2,1,0:T(8,128)(2,1)S(1)} %get-tuple-element.23.blk_ref, f32[256,256]{1,0:T(8,128)S(1)} %get-tuple-element.24.base_ref), custom_call_target="tpu_custom_call" | custom-call | tf_op jit(solution)/shard_map/near_theirs/pallas_call | solution.py:452
  55.8 3.0 %all-to-all-done.1.far_ref = bf16[16,8,1024]{2,1,0:T(8,128)(2,1)S(1)} async-done(((bf16[16,8,1024]{2,1,0:T(8,128)(2,1)}), bf16[16,8,1024]{2,1,0:T(8,128)(2,1)S(1)}, u32[]{:S(2)}, u32[]{:S(2)}) %all-to-all-start.1) | async-done | bytes 262176 | tf_op jit(solution)/shard_map/all_to_all | solution.py:436
  58.9 0.7 %decode.1 = (f32[256,128]{1,0:T(8,128)S(1)}, f32[256,128]{1,0:T(8,128)S(1)}) custom-call(bf16[16,8,1024]{2,1,0:T(8,128)(2,1)S(1)} %all-to-all-done.1.far_ref, bf16[2,512,256]{2,1,0:T(8,128)(2,1)S(1)} %copy-done, f32[256,256]{1,0:T(8,128)S(1)} %near_theirs.1.near_ref), custom_call_target="tpu_custom_call" | custom-call | tf_op jit(solution)/shard_map/decode/pallas_call | solution.py:463
  59.5 0.1 collective-permute-start.6
  59.6 1.3 %collective-permute-done.6 = f32[256,128]{1,0:T(8,128)S(1)} collective-permute-done((f32[256,128]{1,0:T(8,128)S(1)}, f32[256,128]{1,0:T(8,128)S(1)}, u32[]{:S(2)}, u32[]{:S(2)}) %collective-permute-start.6) | collective-permute-done | bytes 131104 | tf_op jit(solution)/shard_map/ppermute | solution.py:475
  61.0 0.7 %add.3 = f32[256,128]{1,0:T(8,128)} add(f32[256,128]{1,0:T(8,128)S(1)} %get-tuple-element.25, f32[256,128]{1,0:T(8,128)S(1)} %collective-permute-done.6) | non-fusion elementwise | flops 32768 | bytes 393216 | tf_op jit(solution)/shard_map/add | solution.py:476
  (5 shorter events, 0.0 us)
Async XLA Ops:
  2.6 9.9 %collective-permute-start = (bf16[4,64,256]{2,1,0:T(8,128)(2,1)S(1)}, bf16[4,64,256]{2,1,0:T(8,128)(2,1)S(1)}, u32[]{:S(2)}, u32[]{:S(2)}) collective-permute-start(bf16[4,64,256]{2,1,0:T(8,128)(2,1)S(1)} %bitcast.10), channel_id=1, source_target_pairs={{0,24},{1,17},{2,26},{3,19},{4,28},{5,21},{6,30},{7,23},{8,16},{9,... | collective-permute-start | bytes 393224 | tf_op jit(solution)/shard_map/ppermute | solution.py:331
  7.8 4.8 %collective-permute-start.1 = (bf16[2,64,256]{2,1,0:T(8,128)(2,1)S(1)}, bf16[2,64,256]{2,1,0:T(8,128)(2,1)S(1)}, u32[]{:S(2)}, u32[]{:S(2)}) collective-permute-start(bf16[2,64,256]{2,1,0:T(8,128)(2,1)S(1)} %bitcast.8), channel_id=1, source_target_pairs={{0,8},{2,10},{4,12},{6,14},{8,0},{10,2},{12,4},{14,6},{16,24},{18,... | collective-permute-start | bytes 196616 | tf_op jit(solution)/shard_map/ppermute | solution.py:332
  12.6 10.2 %collective-permute-start.4 = (bf16[8,64,256]{2,1,0:T(8,128)(2,1)S(1)}, bf16[8,64,256]{2,1,0:T(8,128)(2,1)S(1)}, u32[]{:S(2)}, u32[]{:S(2)}) collective-permute-start(bf16[8,64,256]{2,1,0:T(8,128)(2,1)S(1)} %join.2.refs_0_), channel_id=1, source_target_pairs={{0,6},{2,4},{4,2},{6,0},{8,14},{10,12},{12,10},{14,8},{16,22},{18,... | collective-permute-start | bytes 786440 | tf_op jit(solution)/shard_map/ppermute | solution.py:340
  15.2 11.4 %collective-permute-start.3 = (bf16[8,64,256]{2,1,0:T(8,128)(2,1)S(1)}, bf16[8,64,256]{2,1,0:T(8,128)(2,1)S(1)}, u32[]{:S(2)}, u32[]{:S(2)}) collective-permute-start(bf16[8,64,256]{2,1,0:T(8,128)(2,1)S(1)} %join.2.refs_0_), channel_id=1, source_target_pairs={{0,4},{2,6},{4,0},{6,2},{8,12},{10,14},{12,8},{14,10},{16,20},{18,... | collective-permute-start | bytes 786440 | tf_op jit(solution)/shard_map/ppermute | solution.py:340
  15.7 11.0 %collective-permute-start.2 = (bf16[8,64,256]{2,1,0:T(8,128)(2,1)S(1)}, bf16[8,64,256]{2,1,0:T(8,128)(2,1)S(1)}, u32[]{:S(2)}, u32[]{:S(2)}) collective-permute-start(bf16[8,64,256]{2,1,0:T(8,128)(2,1)S(1)} %join.2.refs_0_), channel_id=1, source_target_pairs={{0,2},{2,0},{4,6},{6,4},{8,10},{10,8},{12,14},{14,12},{16,18},{18,... | collective-permute-start | bytes 786440 | tf_op jit(solution)/shard_map/ppermute | solution.py:340
  26.8 26.6 %collective-permute-start.5 = (bf16[32,64,256]{2,1,0:T(8,128)(2,1)S(1)}, bf16[32,64,256]{2,1,0:T(8,128)(2,1)S(1)}, u32[]{:S(2)}, u32[]{:S(2)}) collective-permute-start(bf16[32,64,256]{2,1,0:T(8,128)(2,1)S(1)} %bitcast.6), channel_id=1, source_target_pairs={{0,1},{1,0},{2,3},{3,2},{4,5},{5,4},{6,7},{7,6},{8,9},{9,8},{10,11... | collective-permute-start | bytes 3145736 | tf_op jit(solution)/shard_map/ppermute | solution.py:397
  26.8 16.6 %all-to-all-start = ((bf16[16,8,1024]{2,1,0:T(8,128)(2,1)}), bf16[16,8,1024]{2,1,0:T(8,128)(2,1)S(1)}, u32[]{:S(2)}, u32[]{:S(2)}) async-start(bf16[16,8,1024]{2,1,0:T(8,128)(2,1)} %get-tuple-element.16), calls=%async_computation | async-start | bytes 524288 | tf_op jit(solution)/shard_map/all_to_all | solution.py:395
  45.8 13.0 %all-to-all-start.1 = ((bf16[16,8,1024]{2,1,0:T(8,128)(2,1)}), bf16[16,8,1024]{2,1,0:T(8,128)(2,1)S(1)}, u32[]{:S(2)}, u32[]{:S(2)}) async-start(bf16[16,8,1024]{2,1,0:T(8,128)(2,1)} %far.1), calls=%async_computation.1 | async-start | bytes 524288 | tf_op jit(solution)/shard_map/all_to_all | solution.py:436
  49.4 9.5 %copy-start = (bf16[2,512,256]{2,1,0:T(8,128)(2,1)S(1)}, bf16[2,512,256]{2,1,0:T(8,128)(2,1)}, u32[]{:S(2)}) copy-start(bf16[2,512,256]{2,1,0:T(8,128)(2,1)} %dec_ref.1) | copy-start | bytes 1572868
  59.5 1.4 %collective-permute-start.6 = (f32[256,128]{1,0:T(8,128)S(1)}, f32[256,128]{1,0:T(8,128)S(1)}, u32[]{:S(2)}, u32[]{:S(2)}) collective-permute-start(f32[256,128]{1,0:T(8,128)S(1)} %get-tuple-element.26), channel_id=1, source_target_pairs={{0,1},{1,0},{2,3},{3,2},{4,5},{5,4},{6,7},{7,6},{8,9},{9,8},{10,11... | collective-permute-start | bytes 393224 | tf_op jit(solution)/shard_map/ppermute | solution.py:475

commit v5 on v4

--- a/solution.py
+++ b/solution.py
@@ -143,6 +143,15 @@
         high = jnp.concatenate([high] * repeat, axis=0)
         low = jnp.concatenate([low] * repeat, axis=0)
         spec_ref[off] = dot_nt(full_hi[...], high) + dot_nt(full_hi[...], low) + dot_nt(full_lo[...], high)
+    if grid_x == 2:
+        for off in (1, 3):
+            spec_ref[off] = spec_ref[off] - spec_ref[0]
+
+
+def times(pair, spec, plane):
+    re, im = pair
+    s_re, s_im = spec[:plane], spec[plane:]
+    return re * s_re - im * s_im, re * s_im + im * s_re
 
 
 def far_kernel(grid_x, coded_ref, fwd_ref, inv_ref, spec_ref, out_ref):
@@ -155,11 +164,23 @@
         coded = coded_ref[:, :, cols].reshape(owners * rows, step)
         coded = jnp.concatenate([coded, coded], axis=0)
         data = [dot_nn(fwd_ref[x], coded) for x in range(grid_x)]
+        shared = []
+        if grid_x == 2:
+            for tile in range(step // LANES):
+                lanes = slice(tile * LANES, (tile + 1) * LANES)
+                first = data[0][:plane, lanes], data[0][plane:, lanes]
+                second = data[1][:plane, lanes], data[1][plane:, lanes]
+                base = times((first[0] + second[0], first[1] + second[1]), spec_ref[0], plane)
+                below, above = times(second, spec_ref[3], plane), times(first, spec_ref[1], plane)
+                shared.append([jnp.concatenate([base[0] + p[0], base[1] + p[1]], axis=0) for p in (below, above)])
         total = None
         for x in range(grid_x):
             tiles = []
             for tile in range(step // LANES):
                 lanes = slice(tile * LANES, (tile + 1) * LANES)
+                if grid_x == 2:
+                    tiles.append(shared[tile][x])
+                    continue
                 re = im = None
                 for s in range(grid_x):
                     off = (x - s) % double_x

time: 62 us -> 62 us (level)
  no operation moved by 1% of the time
where the time goes in v5:
time: 62 us; the launch traced here: 61.6 us
  waiting for transfers between devices  27.8 us (45%)
  starting transfers between devices  18.8 us (30%)
  Pallas kernels  14.2 us (23%)
  other arithmetic  0.67 us (1%)
    ppermute x3, waiting for transfers between devices, gather_shares(): lax.ppermute(held, 'box', [(i, i ^ delta * rest) for i in range(size)])  10.6 us
    all_to_all x1, waiting for transfers between devices, whole_product(): lax.all_to_all(coded, 'box', split_axis=0, concat_axis=0, tiled=True)  8.07 us
    all_to_all x1, starting transfers between devices, whole_product(): lax.all_to_all(coded, 'box', split_axis=0, concat_axis=0, tiled=True)  6.4 us
    ppermute x1, starting transfers between devices, gather_shares(): whole = lax.ppermute(boxes, ('box', 'dir'), pairs)  5.14 us
    ppermute x1, waiting for transfers between devices, gather_shares(): third = lax.ppermute(share, 'box', [(i, i ^ rest) for i in range(size)])  4.76 us
    pallas_call x1, Pallas kernels, whole_product(): pl.pallas_call(functools.partial(near_mine_kernel, per_box), out_shape=(p...  3.98 us
    ppermute x3, starting transfers between devices, gather_shares(): lax.ppermute(held, 'box', [(i, i ^ delta * rest) for i in range(size)])  3.55 us
    all_to_all x1, starting transfers between devices, whole_product(): lax.all_to_all(far, 'box', split_axis=0, concat_axis=0, tiled=True)  3.55 us
  transfers between devices with their start and end apart: 9, of which 7 were waited for; matrix products, arithmetic and copies ran while one was open for 0% of the time, Pallas kernels for 18%

profile of v5, /device:TPU:0, one launch (start us, length us, event | category | flops | bytes accessed | tf_op | source)
XLA Modules:
  0.0 61.6 jit_solution(1408879365473477673)
XLA Ops:
  0.0 2.6 %encode.1 = (bf16[16,8,1024]{2,1,0:T(8,128)(2,1)}, bf16[256,256]{1,0:T(8,128)(2,1)S(1)}, bf16[128,256]{1,0:T(8,128)(2,1)S(1)}) custom-call(bf16[256,256]{1,0:T(8,128)(2,1)} %bitcast.11, bf16[2,512,256]{2,1,0:T(8,128)(2,1)} %enc_hbm.1), custom_call_target="tpu_custom_call" | custom-call | tf_op jit(solution)/shard_map/encode/pallas_call | solution.py:398
  2.6 5.1 %collective-permute-start = (bf16[4,64,256]{2,1,0:T(8,128)(2,1)S(1)}, bf16[4,64,256]{2,1,0:T(8,128)(2,1)S(1)}, u32[]{:S(2)}, u32[]{:S(2)}) collective-permute-start(bf16[4,64,256]{2,1,0:T(8,128)(2,1)S(1)} %bitcast.10), channel_id=1, source_target_pairs={{0,24},{1,17},{2,26},{3,19},{4,28},{5,21},{6,30},{7,23},{8,16},{9,... | collective-permute-start | bytes 393224 | tf_op jit(solution)/shard_map/ppermute | solution.py:352
  7.8 4.8 %collective-permute-done.1.refs_2_ = bf16[2,64,256]{2,1,0:T(8,128)(2,1)S(1)} collective-permute-done((bf16[2,64,256]{2,1,0:T(8,128)(2,1)S(1)}, bf16[2,64,256]{2,1,0:T(8,128)(2,1)S(1)}, u32[]{:S(2)}, u32[]{:S(2)}) %collective-permute-start.1) | collective-permute-done | bytes 65568 | tf_op jit(solution)/shard_map/ppermute | solution.py:353
  12.6 2.6 %collective-permute-start.4 = (bf16[8,64,256]{2,1,0:T(8,128)(2,1)S(1)}, bf16[8,64,256]{2,1,0:T(8,128)(2,1)S(1)}, u32[]{:S(2)}, u32[]{:S(2)}) collective-permute-start(bf16[8,64,256]{2,1,0:T(8,128)(2,1)S(1)} %join.2.refs_0_), channel_id=1, source_target_pairs={{0,6},{2,4},{4,2},{6,0},{8,14},{10,12},{12,10},{14,8},{16,22},{18,... | collective-permute-start | bytes 786440 | tf_op jit(solution)/shard_map/ppermute | solution.py:361
  15.2 0.5 collective-permute-start.3
  15.7 0.4 collective-permute-start.2
  16.1 6.6 %collective-permute-done.4.refs_3_ = bf16[8,64,256]{2,1,0:T(8,128)(2,1)S(1)} collective-permute-done((bf16[8,64,256]{2,1,0:T(8,128)(2,1)S(1)}, bf16[8,64,256]{2,1,0:T(8,128)(2,1)S(1)}, u32[]{:S(2)}, u32[]{:S(2)}) %collective-permute-start.4) | collective-permute-done | bytes 262176 | tf_op jit(solution)/shard_map/ppermute | solution.py:361
  22.8 3.8 %collective-permute-done.3.refs_2_ = bf16[8,64,256]{2,1,0:T(8,128)(2,1)S(1)} collective-permute-done((bf16[8,64,256]{2,1,0:T(8,128)(2,1)S(1)}, bf16[8,64,256]{2,1,0:T(8,128)(2,1)S(1)}, u32[]{:S(2)}, u32[]{:S(2)}) %collective-permute-start.3) | collective-permute-done | bytes 262176 | tf_op jit(solution)/shard_map/ppermute | solution.py:361
  26.6 0.1 collective-permute-done.2.refs_1_
  26.7 0.1 join.3
  26.8 0.1 collective-permute-start.5
  26.8 6.4 %all-to-all-start = ((bf16[16,8,1024]{2,1,0:T(8,128)(2,1)}), bf16[16,8,1024]{2,1,0:T(8,128)(2,1)S(1)}, u32[]{:S(2)}, u32[]{:S(2)}) async-start(bf16[16,8,1024]{2,1,0:T(8,128)(2,1)} %get-tuple-element.16), calls=%async_computation | async-start | bytes 524288 | tf_op jit(solution)/shard_map/all_to_all | solution.py:416
  33.2 2.1 %tables.1 = (bf16[2,256,256]{2,1,0:T(8,128)(2,1)S(1)}, bf16[2,2,128,256]{3,2,1,0:T(8,128)(2,1)S(1)}, f32[4,256,128]{2,1,0:T(8,128)S(1)}, s32[8,128]{1,0:T(8,128)S(1)}) custom-call(s32[4,14]{1,0:T(4,128)} %list_hbm.1, s32[4,14]{1,0:T(4,128)} %mask_hbm.1, s32[1,64]{1,0:T(1,128)} %bitcast.12, f32[32,2,4,128]{3,2,1,0:T(4,128)} %kern_hbm.1, ...), custom_call_target="tpu_custom_call" | custom-call | tf_op jit(solution)/shard_map/tables/pallas_call | solution.py:426
  35.4 8.1 %all-to-all-done.coded_ref = bf16[16,8,1024]{2,1,0:T(8,128)(2,1)S(1)} async-done(((bf16[16,8,1024]{2,1,0:T(8,128)(2,1)}), bf16[16,8,1024]{2,1,0:T(8,128)(2,1)S(1)}, u32[]{:S(2)}, u32[]{:S(2)}) %all-to-all-start) | async-done | bytes 262176 | tf_op jit(solution)/shard_map/all_to_all | solution.py:416
  43.5 2.3 %far.1 = bf16[16,8,1024]{2,1,0:T(8,128)(2,1)} custom-call(bf16[16,8,1024]{2,1,0:T(8,128)(2,1)S(1)} %all-to-all-done.coded_ref, bf16[2,256,256]{2,1,0:T(8,128)(2,1)S(1)} %get-tuple-element.17.fwd_ref, bf16[2,2,128,256]{3,2,1,0:T(8,128)(2,1)S(1)} %get-tuple-element.18.inv_ref, f32[4,256,128]{2,1,0:T(8,128)S(1)} %get-tuple-element.19.spec_ref), custom_call_target="tpu_custom_call" | custom-call | tf_op jit(solution)/shard_map/far/pallas_call | solution.py:449
  45.7 3.5 %all-to-all-start.1 = ((bf16[16,8,1024]{2,1,0:T(8,128)(2,1)}), bf16[16,8,1024]{2,1,0:T(8,128)(2,1)S(1)}, u32[]{:S(2)}, u32[]{:S(2)}) async-start(bf16[16,8,1024]{2,1,0:T(8,128)(2,1)} %far.1), calls=%async_computation.1 | async-start | bytes 524288 | tf_op jit(solution)/shard_map/all_to_all | solution.py:457
  49.3 0.0 copy-start
  49.3 4.0 %near_mine.1 = (bf16[57,2,256,256]{3,2,1,0:T(8,128)(2,1)S(1)}, f32[256,256]{1,0:T(8,128)S(1)}) custom-call(s32[8,128]{1,0:T(8,128)S(1)} %get-tuple-element.20.order_ref, bf16[32,64,256]{2,1,0:T(8,128)(2,1)S(1)} %bitcast.7, bf16[4,14,2,256,256]{4,3,2,1,0:T(8,128)(2,1)} %blocks_hbm.1), custom_call_target="tpu_custom_call" | custom-call | tf_op jit(solution)/shard_map/near_mine/pallas_call | solution.py:461
  53.3 2.4 %near_theirs.1.near_ref = f32[256,256]{1,0:T(8,128)S(1)} custom-call(s32[8,128]{1,0:T(8,128)S(1)} %get-tuple-element.20.order_ref, bf16[32,64,256]{2,1,0:T(8,128)(2,1)S(1)} %collective-permute-done.5.src_ref, bf16[57,2,256,256]{3,2,1,0:T(8,128)(2,1)S(1)} %get-tuple-element.23.blk_ref, f32[256,256]{1,0:T(8,128)S(1)} %get-tuple-element.24.base_ref), custom_call_target="tpu_custom_call" | custom-call | tf_op jit(solution)/shard_map/near_theirs/pallas_call | solution.py:473
  55.7 3.0 %all-to-all-done.1.far_ref = bf16[16,8,1024]{2,1,0:T(8,128)(2,1)S(1)} async-done(((bf16[16,8,1024]{2,1,0:T(8,128)(2,1)}), bf16[16,8,1024]{2,1,0:T(8,128)(2,1)S(1)}, u32[]{:S(2)}, u32[]{:S(2)}) %all-to-all-start.1) | async-done | bytes 262176 | tf_op jit(solution)/shard_map/all_to_all | solution.py:457
  58.8 0.7 %decode.1 = (f32[256,128]{1,0:T(8,128)S(1)}, f32[256,128]{1,0:T(8,128)S(1)}) custom-call(bf16[16,8,1024]{2,1,0:T(8,128)(2,1)S(1)} %all-to-all-done.1.far_ref, bf16[2,512,256]{2,1,0:T(8,128)(2,1)S(1)} %copy-done, f32[256,256]{1,0:T(8,128)S(1)} %near_theirs.1.near_ref), custom_call_target="tpu_custom_call" | custom-call | tf_op jit(solution)/shard_map/decode/pallas_call | solution.py:484
  59.5 0.1 collective-permute-start.6
  59.6 1.3 %collective-permute-done.6 = f32[256,128]{1,0:T(8,128)S(1)} collective-permute-done((f32[256,128]{1,0:T(8,128)S(1)}, f32[256,128]{1,0:T(8,128)S(1)}, u32[]{:S(2)}, u32[]{:S(2)}) %collective-permute-start.6) | collective-permute-done | bytes 131104 | tf_op jit(solution)/shard_map/ppermute | solution.py:496
  60.9 0.7 %add.3 = f32[256,128]{1,0:T(8,128)} add(f32[256,128]{1,0:T(8,128)S(1)} %get-tuple-element.25, f32[256,128]{1,0:T(8,128)S(1)} %collective-permute-done.6) | non-fusion elementwise | flops 32768 | bytes 393216 | tf_op jit(solution)/shard_map/add | solution.py:497
  (5 shorter events, 0.0 us)
Async XLA Ops:
  2.6 9.9 %collective-permute-start = (bf16[4,64,256]{2,1,0:T(8,128)(2,1)S(1)}, bf16[4,64,256]{2,1,0:T(8,128)(2,1)S(1)}, u32[]{:S(2)}, u32[]{:S(2)}) collective-permute-start(bf16[4,64,256]{2,1,0:T(8,128)(2,1)S(1)} %bitcast.10), channel_id=1, source_target_pairs={{0,24},{1,17},{2,26},{3,19},{4,28},{5,21},{6,30},{7,23},{8,16},{9,... | collective-permute-start | bytes 393224 | tf_op jit(solution)/shard_map/ppermute | solution.py:352
  7.8 4.8 %collective-permute-start.1 = (bf16[2,64,256]{2,1,0:T(8,128)(2,1)S(1)}, bf16[2,64,256]{2,1,0:T(8,128)(2,1)S(1)}, u32[]{:S(2)}, u32[]{:S(2)}) collective-permute-start(bf16[2,64,256]{2,1,0:T(8,128)(2,1)S(1)} %bitcast.8), channel_id=1, source_target_pairs={{0,8},{2,10},{4,12},{6,14},{8,0},{10,2},{12,4},{14,6},{16,24},{18,... | collective-permute-start | bytes 196616 | tf_op jit(solution)/shard_map/ppermute | solution.py:353
  12.6 10.2 %collective-permute-start.4 = (bf16[8,64,256]{2,1,0:T(8,128)(2,1)S(1)}, bf16[8,64,256]{2,1,0:T(8,128)(2,1)S(1)}, u32[]{:S(2)}, u32[]{:S(2)}) collective-permute-start(bf16[8,64,256]{2,1,0:T(8,128)(2,1)S(1)} %join.2.refs_0_), channel_id=1, source_target_pairs={{0,6},{2,4},{4,2},{6,0},{8,14},{10,12},{12,10},{14,8},{16,22},{18,... | collective-permute-start | bytes 786440 | tf_op jit(solution)/shard_map/ppermute | solution.py:361
  15.2 11.4 %collective-permute-start.3 = (bf16[8,64,256]{2,1,0:T(8,128)(2,1)S(1)}, bf16[8,64,256]{2,1,0:T(8,128)(2,1)S(1)}, u32[]{:S(2)}, u32[]{:S(2)}) collective-permute-start(bf16[8,64,256]{2,1,0:T(8,128)(2,1)S(1)} %join.2.refs_0_), channel_id=1, source_target_pairs={{0,4},{2,6},{4,0},{6,2},{8,12},{10,14},{12,8},{14,10},{16,20},{18,... | collective-permute-start | bytes 786440 | tf_op jit(solution)/shard_map/ppermute | solution.py:361
  15.7 11.0 %collective-permute-start.2 = (bf16[8,64,256]{2,1,0:T(8,128)(2,1)S(1)}, bf16[8,64,256]{2,1,0:T(8,128)(2,1)S(1)}, u32[]{:S(2)}, u32[]{:S(2)}) collective-permute-start(bf16[8,64,256]{2,1,0:T(8,128)(2,1)S(1)} %join.2.refs_0_), channel_id=1, source_target_pairs={{0,2},{2,0},{4,6},{6,4},{8,10},{10,8},{12,14},{14,12},{16,18},{18,... | collective-permute-start | bytes 786440 | tf_op jit(solution)/shard_map/ppermute | solution.py:361
  26.8 26.6 %collective-permute-start.5 = (bf16[32,64,256]{2,1,0:T(8,128)(2,1)S(1)}, bf16[32,64,256]{2,1,0:T(8,128)(2,1)S(1)}, u32[]{:S(2)}, u32[]{:S(2)}) collective-permute-start(bf16[32,64,256]{2,1,0:T(8,128)(2,1)S(1)} %bitcast.6), channel_id=1, source_target_pairs={{0,1},{1,0},{2,3},{3,2},{4,5},{5,4},{6,7},{7,6},{8,9},{9,8},{10,11... | collective-permute-start | bytes 3145736 | tf_op jit(solution)/shard_map/ppermute | solution.py:418
  26.8 16.6 %all-to-all-start = ((bf16[16,8,1024]{2,1,0:T(8,128)(2,1)}), bf16[16,8,1024]{2,1,0:T(8,128)(2,1)S(1)}, u32[]{:S(2)}, u32[]{:S(2)}) async-start(bf16[16,8,1024]{2,1,0:T(8,128)(2,1)} %get-tuple-element.16), calls=%async_computation | async-start | bytes 524288 | tf_op jit(solution)/shard_map/all_to_all | solution.py:416
  45.7 13.0 %all-to-all-start.1 = ((bf16[16,8,1024]{2,1,0:T(8,128)(2,1)}), bf16[16,8,1024]{2,1,0:T(8,128)(2,1)S(1)}, u32[]{:S(2)}, u32[]{:S(2)}) async-start(bf16[16,8,1024]{2,1,0:T(8,128)(2,1)} %far.1), calls=%async_computation.1 | async-start | bytes 524288 | tf_op jit(solution)/shard_map/all_to_all | solution.py:457
  49.3 9.5 %copy-start = (bf16[2,512,256]{2,1,0:T(8,128)(2,1)S(1)}, bf16[2,512,256]{2,1,0:T(8,128)(2,1)}, u32[]{:S(2)}) copy-start(bf16[2,512,256]{2,1,0:T(8,128)(2,1)} %dec_ref.1) | copy-start | bytes 1572868
  59.5 1.4 %collective-permute-start.6 = (f32[256,128]{1,0:T(8,128)S(1)}, f32[256,128]{1,0:T(8,128)S(1)}, u32[]{:S(2)}, u32[]{:S(2)}) collective-permute-start(f32[256,128]{1,0:T(8,128)S(1)} %get-tuple-element.26), channel_id=1, source_target_pairs={{0,1},{1,0},{2,3},{3,2},{4,5},{5,4},{6,7},{7,6},{8,9},{9,8},{10,11... | collective-permute-start | bytes 393224 | tf_op jit(solution)/shard_map/ppermute | solution.py:496
